TPU v7x, 32 devices: a whole 2x2x4 slice. The times are simulated.
32 devices in a mesh: group: 2 (over x), azim: 16 (over z, y, core).
Axes of the slice: x: 2, y: 2, z: 4, core: 2. Of those that a mesh axis runs over, the one named last changes fastest.
Arguments:
- field: bfloat16 [704, 8, 8, 640], P(('group', 'azim')), parts along dimension 0, may hold values from -6 to 6
- jacobian: bfloat16 [5, 8, 2, 320, 320], P(None, None, None, 'azim'), may hold values from -0.109375 to 0.109375
- coupling: int32 [16, 5], replicated, may hold values 0 or 1
Outputs:
- transferred: bfloat16 [704, 8, 8, 640], P(('group', 'azim')), parts along dimension 0
There are 2 independent parts, one for each index of `group`. A program takes and returns all parts, laid end to end along the dimension named above; an argument that names none is the same for every part. Nothing has to cross between parts.
All inputs are finite; a program needn't handle non-finite values.
Results may differ from a plain program's by a relative error of at most 0.0049.
Values may be sent and summed in bfloat16 or wider, within the bound.
No kernel may reach another device: no remote copies, remote signals or barrier semaphores. Data moves between devices by JAX's collectives and lax.ppermute only.
A program may use at most 128 MiB of HBM per device.

v0:
```python
import math

import jax
import jax.numpy as jnp
import numpy as np
from jax import lax
from jax.sharding import PartitionSpec as P

BLADES = 22


def twiddles(row_count, col_count, modulus):
    rows_iota = jnp.arange(row_count, dtype=jnp.int32)[:, None]
    cols_iota = jnp.arange(col_count, dtype=jnp.int32)[None, :]
    phase = rows_iota * cols_iota % modulus
    angle = phase.astype(jnp.float32) * (2.0 * math.pi / modulus)
    return (jnp.cos(angle), jnp.sin(angle))


def real_form(jac_item):
    jac_real = jac_item[:, 0]
    jac_imag = jac_item[:, 1]
    upper = jnp.concatenate([jac_real, -jac_imag], axis=2)
    lower = jnp.concatenate([jac_imag, jac_real], axis=2)
    return jnp.concatenate([upper, lower], axis=1)


def shards(field, jacobian, coupling):
    local_stations, axial_count, freq_count, full_width = field.shape
    node_count = lax.axis_size("azim")
    item_count = axial_count * freq_count
    per_device = item_count // node_count
    half_width = full_width // 2
    order_count = jacobian.shape[0]
    precise = lax.Precision.HIGH
    flattened = field.reshape(local_stations, item_count, full_width)
    columns = lax.all_to_all(flattened, "azim", split_axis=1, concat_axis=0, tiled=True)
    targets = np.arange(node_count * per_device) % freq_count
    outgoing = jnp.take(jacobian, jnp.asarray(targets, dtype=jnp.int32), axis=1)
    local_jac = lax.all_to_all(outgoing, "azim", split_axis=1, concat_axis=3, tiled=True)
    stations = columns.shape[0]
    passage = stations // BLADES
    norm_scale = 1.0 / math.sqrt(stations)
    cos_blade, sin_blade = twiddles(BLADES, BLADES, BLADES)
    cos_twist, sin_twist = twiddles(BLADES, passage, stations)
    cos_pass, sin_pass = twiddles(passage, passage, passage)
    twist_c = cos_twist[:, :, None]
    twist_s = sin_twist[:, :, None]
    gate_table = coupling.astype(jnp.bfloat16)

    def transform(position, buffer):
        sample = lax.dynamic_index_in_dim(columns, position, 1, keepdims=False)
        values = sample.astype(jnp.float32).reshape(BLADES, passage, full_width)
        first_c = jnp.einsum("rb,bav->rav", cos_blade, values, precision=precise)
        first_s = jnp.einsum("rb,bav->rav", sin_blade, values, precision=precise)
        part_real = first_c[..., :half_width] + first_s[..., half_width:]
        part_imag = first_c[..., half_width:] - first_s[..., :half_width]
        turned = jnp.concatenate(
            [twist_c * part_real + twist_s * part_imag, twist_c * part_imag - twist_s * part_real],
            axis=-1,
        )
        second_c = jnp.einsum("qa,rav->qrv", cos_pass, turned, precision=precise)
        second_s = jnp.einsum("qa,rav->qrv", sin_pass, turned, precision=precise)
        modes = (
            jnp.concatenate(
                [
                    second_c[..., :half_width] + second_s[..., half_width:],
                    second_c[..., half_width:] - second_s[..., :half_width],
                ],
                axis=-1,
            )
            * norm_scale
        ).astype(jnp.bfloat16)
        operator = real_form(lax.dynamic_index_in_dim(local_jac, position, 1, keepdims=False))
        coupled = jnp.zeros((passage, BLADES, full_width), jnp.float32)
        for order_idx in range(order_count):
            moved = (
                jnp.roll(modes, -(order_idx - order_count // 2), axis=0)
                * gate_table[:, order_idx][:, None, None]
            )
            coupled = coupled + jnp.einsum(
                "qri,oi->qro", moved, operator[order_idx], preferred_element_type=jnp.float32
            )
        third_c = jnp.einsum("qa,qrv->rav", cos_pass, coupled, precision=precise)
        third_s = jnp.einsum("qa,qrv->rav", sin_pass, coupled, precision=precise)
        back_real = third_c[..., :half_width] - third_s[..., half_width:]
        back_imag = third_c[..., half_width:] + third_s[..., :half_width]
        spun = jnp.concatenate(
            [twist_c * back_real - twist_s * back_imag, twist_c * back_imag + twist_s * back_real],
            axis=-1,
        )
        last_c = jnp.einsum("rb,rav->bav", cos_blade, spun, precision=precise)
        last_s = jnp.einsum("rb,rav->bav", sin_blade, spun, precision=precise)
        restored = (
            jnp.concatenate(
                [
                    last_c[..., :half_width] - last_s[..., half_width:],
                    last_c[..., half_width:] + last_s[..., :half_width],
                ],
                axis=-1,
            )
            * norm_scale
        )
        result = restored.reshape(stations, full_width).astype(jnp.bfloat16)
        return lax.dynamic_update_index_in_dim(buffer, result, position, 1)

    initial = jnp.zeros((stations, per_device, full_width), jnp.bfloat16)
    finished = lax.fori_loop(0, per_device, transform, initial)
    returned = lax.all_to_all(finished, "azim", split_axis=0, concat_axis=1, tiled=True)
    return returned.reshape(local_stations, axial_count, freq_count, full_width)


def solution(mesh):
    placed = (P(("group", "azim"), None, None, None), P(None, None, None, "azim", None), P())
    return jax.shard_map(
        shards,
        mesh=mesh,
        in_specs=placed,
        out_specs=P(("group", "azim"), None, None, None),
        check_vma=False,
    )
```

profile of v0, /device:TPU:1, one launch (start us, length us, event | category | flops | bytes accessed | tf_op | source)
XLA Modules:
  0.0 432.2 jit_solution(5272978858724558747)
XLA Ops:
  0.0 3.9 copy.112
  3.9 7.5 %all-to-all-start = ((bf16[22,64,640]{2,0,1:T(8,128)(2,1)}), bf16[22,64,640]{2,0,1:T(8,128)(2,1)S(1)}, u32[]{:S(2)}, u32[]{:S(2)}) async-start(bf16[22,64,640]{2,0,1:T(8,128)(2,1)} %bitcast.173), calls=%async_computation | async-start | bytes 3932160 | tf_op jit(solution)/shard_map/all_to_all | solution.py:37
  11.4 21.1 %gather_fusion = bf16[64,5,2,20,320]{4,2,3,1,0:T(2,128)(2,1)} fusion(bf16[5,8,2,20,320]{4,2,3,1,0:T(2,128)(2,1)S(1)} %copy-done, s32[1024]{0:T(1024)S(1)} %pad_clamp_fusion), kind=kCustom, calls=%fused_computation | custom fusion | bytes 16384256 | tf_op jit(solution)/shard_map/jit(_take)/gather | solution.py:39
  32.6 18.0 %all-to-all-done = bf16[22,64,640]{2,0,1:T(8,128)(2,1)S(1)} async-done(((bf16[22,64,640]{2,0,1:T(8,128)(2,1)}), bf16[22,64,640]{2,0,1:T(8,128)(2,1)S(1)}, u32[]{:S(2)}, u32[]{:S(2)}) %all-to-all-start) | async-done | bytes 1802272 | tf_op jit(solution)/shard_map/all_to_all | solution.py:37
  50.6 10.5 %all-to-all-start.1 = ((bf16[5,64,2,20,320]{4,2,3,0,1:T(2,128)(2,1)}), bf16[5,64,2,20,320]{4,2,3,0,1:T(2,128)(2,1)}, u32[]{:S(2)}, u32[]{:S(2)}) async-start(bf16[5,64,2,20,320]{4,2,3,0,1:T(2,128)(2,1)} %bitcast.171), calls=%async_computation.1 | async-start | bytes 19660800 | tf_op jit(solution)/shard_map/all_to_all | solution.py:40
  62.0 175.3 %all-to-all-done.1 = bf16[5,64,2,20,320]{4,2,3,0,1:T(2,128)(2,1)} async-done(((bf16[5,64,2,20,320]{4,2,3,0,1:T(2,128)(2,1)}), bf16[5,64,2,20,320]{4,2,3,0,1:T(2,128)(2,1)}, u32[]{:S(2)}, u32[]{:S(2)}) %all-to-all-start.1) | async-done | bytes 8192032 | tf_op jit(solution)/shard_map/all_to_all | solution.py:40
  237.3 9.3 %copy.115 = bf16[5,16,4,2,20,320]{5,3,4,1,2,0:T(2,128)(2,1)} copy(bf16[5,16,4,2,20,320]{5,3,4,0,2,1:T(2,128)(2,1)} %bitcast.6) | data formatting | bytes 16384000 | tf_op jit(solution)/shard_map/all_to_all | solution.py:40
  246.5 96.6 %while.15 = (s32[]{:T(128)}, bf16[352,4,640]{2,0,1:T(8,128)(2,1)}, bf16[352,4,640]{2,0,1:T(8,128)(2,1)S(1)}, bf16[16,5]{0,1:T(8,128)(2,1)S(1)}, bf16[5,4,2,320,320]{4,2,3,1,0:T(2,128)(2,1)}, /*index=5*/s32[]{:T(128)}) while((s32[]{:T(128)}, bf16[352,4,640]{2,0,1:T(8,128)(2,1)}, bf16[352,4,640]{2,0,1:T(8,128)(2,1)S(1)}, ...), condition=%wide.region_1.2_spmd.clone.clone, body=%wide.region_0.1_spmd.clone.clone.sunk | while | flops 1674994944 | bytes 79102776 | solution.py:108
  246.7 3.4 constant_dynamic-slice_fusion.4
  250.8 6.1 %maximum_maximum_fusion.2 = bf16[5,640,640]{2,1,0:T(8,128)(2,1)S(1)} fusion(bf16[5,320,320]{2,1,0:T(8,128)(2,1)S(1)} %get-tuple-element.401, bf16[5,320,320]{2,1,0:T(8,128)(2,1)S(1)} %get-tuple-element.402, bf16[5,320,320]{2,1,0:T(8,128)(2,1)S(1)} %fusion.160), kind=kLoop, calls=%fused_computation.7.clone.1 | loop fusion | flops 16384000 | bytes 7168000 | tf_op jit(solution)/shard_map/while/body/eval_jaxpr/concatenate | solution.py:25
  269.7 1.0 fusion.168
  270.8 3.4 constant_dynamic-slice_fusion.4
  274.9 6.1 %maximum_maximum_fusion.2 = bf16[5,640,640]{2,1,0:T(8,128)(2,1)S(1)} fusion(bf16[5,320,320]{2,1,0:T(8,128)(2,1)S(1)} %get-tuple-element.401, bf16[5,320,320]{2,1,0:T(8,128)(2,1)S(1)} %get-tuple-element.402, bf16[5,320,320]{2,1,0:T(8,128)(2,1)S(1)} %fusion.160), kind=kLoop, calls=%fused_computation.7.clone.1 | loop fusion | flops 16384000 | bytes 7168000 | tf_op jit(solution)/shard_map/while/body/eval_jaxpr/concatenate | solution.py:25
  293.9 1.0 fusion.168
  295.0 3.4 constant_dynamic-slice_fusion.4
  299.1 6.1 %maximum_maximum_fusion.2 = bf16[5,640,640]{2,1,0:T(8,128)(2,1)S(1)} fusion(bf16[5,320,320]{2,1,0:T(8,128)(2,1)S(1)} %get-tuple-element.401, bf16[5,320,320]{2,1,0:T(8,128)(2,1)S(1)} %get-tuple-element.402, bf16[5,320,320]{2,1,0:T(8,128)(2,1)S(1)} %fusion.160), kind=kLoop, calls=%fused_computation.7.clone.1 | loop fusion | flops 16384000 | bytes 7168000 | tf_op jit(solution)/shard_map/while/body/eval_jaxpr/concatenate | solution.py:25
  318.0 1.0 fusion.168
  319.1 3.4 constant_dynamic-slice_fusion.4
  323.2 6.1 %maximum_maximum_fusion.2 = bf16[5,640,640]{2,1,0:T(8,128)(2,1)S(1)} fusion(bf16[5,320,320]{2,1,0:T(8,128)(2,1)S(1)} %get-tuple-element.401, bf16[5,320,320]{2,1,0:T(8,128)(2,1)S(1)} %get-tuple-element.402, bf16[5,320,320]{2,1,0:T(8,128)(2,1)S(1)} %fusion.160), kind=kLoop, calls=%fused_computation.7.clone.1 | loop fusion | flops 16384000 | bytes 7168000 | tf_op jit(solution)/shard_map/while/body/eval_jaxpr/concatenate | solution.py:25
  342.2 1.0 fusion.168
  343.1 2.4 copy.118
  345.6 84.3 %all_to_all.51 = bf16[352,4,640]{2,1,0:T(4,128)(2,1)S(1)} all-to-all(bf16[352,4,640]{2,1,0:T(4,128)(2,1)S(1)} %copy.118), channel_id=1, replica_groups=mesh['group'=2,'azim'=16] {'azim'}, dimensions={0} | all-to-all | bytes 3604480 | tf_op jit(solution)/shard_map/all_to_all | solution.py:109
  429.8 0.9 copy.119
  430.7 1.4 reshape.120
  (157 shorter events, 54.8 us)
Async XLA Ops:
  0.0 11.4 %copy-start = (bf16[5,8,2,20,320]{4,2,3,1,0:T(2,128)(2,1)S(1)}, bf16[5,8,2,20,320]{4,2,3,1,0:T(2,128)(2,1)}, u32[]{:S(2)}) copy-start(bf16[5,8,2,20,320]{4,2,3,1,0:T(2,128)(2,1)} %param.7) | copy-start | bytes 3072004
  3.9 7.5 %copy-start.3 = (s32[64]{0:T(128)S(1)}, s32[64]{0:T(128)}, u32[]{:S(2)}) copy-start(s32[64]{0:T(128)} %constant.113) | copy-start | bytes 772
  3.9 46.7 %all-to-all-start = ((bf16[22,64,640]{2,0,1:T(8,128)(2,1)}), bf16[22,64,640]{2,0,1:T(8,128)(2,1)S(1)}, u32[]{:S(2)}, u32[]{:S(2)}) async-start(bf16[22,64,640]{2,0,1:T(8,128)(2,1)} %bitcast.173), calls=%async_computation | async-start | bytes 3932160 | tf_op jit(solution)/shard_map/all_to_all | solution.py:37
  50.6 10.5 %copy-start.2 = (s32[16,5]{0,1:T(8,128)S(1)}, s32[16,5]{0,1:T(8,128)}, u32[]{:S(2)}) copy-start(s32[16,5]{0,1:T(8,128)} %param.8) | copy-start | bytes 964
  50.6 186.7 %all-to-all-start.1 = ((bf16[5,64,2,20,320]{4,2,3,0,1:T(2,128)(2,1)}), bf16[5,64,2,20,320]{4,2,3,0,1:T(2,128)(2,1)}, u32[]{:S(2)}, u32[]{:S(2)}) async-start(bf16[5,64,2,20,320]{4,2,3,0,1:T(2,128)(2,1)} %bitcast.171), calls=%async_computation.1 | async-start | bytes 19660800 | tf_op jit(solution)/shard_map/all_to_all | solution.py:40
  429.8 2.3 copy-start.1
where the time goes:
time: 433 us; the launch traced here: 432 us
  waiting for transfers between devices  193 us (45%)
  blocking collectives  84.3 us (19%)
  local copies, waits for them, and re-layouts  61.2 us (14%)
  other arithmetic  41.7 us (10%)
  matrix products  32.7 us (8%)
  starting transfers between devices  17.9 us (4%)
    all_to_all x1, waiting for transfers between devices, shards(): lax.all_to_all(outgoing, 'azim', split_axis=1, concat_axis=3, tiled=True)  175 us
    all_to_all x1, blocking collectives, shards(): lax.all_to_all(finished, 'azim', split_axis=0, concat_axis=1, tiled=True)  84.3 us
    concatenate x4, other arithmetic, real_form(): return jnp.concatenate([upper, lower], axis=1)  24.3 us
    gather x1, local copies, waits for them, and re-layouts, shards(): outgoing = jnp.take(jacobian, jnp.asarray(targets, dtype=jnp.int32), axis=1)  21.1 us
    all_to_all x1, waiting for transfers between devices, shards(): lax.all_to_all(flattened, 'azim', split_axis=1, concat_axis=0, tiled=True)  18 us
    dynamic_slice x8, local copies, waits for them, and re-layouts, transform(): lax.dynamic_index_in_dim(local_jac, position, 1, keepdims=False)  15 us
    dot_general x20, matrix products, transform(): jnp.einsum('qri,oi->qro', moved, operator[order_idx], preferred_element_t...  13.5 us
    all_to_all x1, starting transfers between devices, shards(): lax.all_to_all(outgoing, 'azim', split_axis=1, concat_axis=3, tiled=True)  10.5 us
  transfers between devices with their start and end apart: 2, of which 2 were waited for; matrix products, arithmetic and copies ran while one was open for 5% of the time, Pallas kernels for 0%

commit v1 on v0

v1 whole, which is shorter than its diff:
```python
import functools
import math

import jax
import jax.numpy as jnp
import ml_dtypes
import numpy as np
from jax import lax
from jax.experimental import pallas as pl
from jax.experimental.pallas import tpu as pltpu
from jax.sharding import Mesh
from jax.sharding import PartitionSpec as P

BLADES = 22
ROWS = 24


def round_up(value, multiple):
    return -(-value // multiple) * multiple


def windows(items):
    spans = []
    for item in range(items):
        first = BLADES * item
        low = first // 8 * 8
        spans.append((low, round_up(first + BLADES, 8), first - low))
    return spans


@functools.lru_cache(maxsize=None)
def phases(stations):
    index = np.arange(stations, dtype=np.int64)
    angle = (index[:, None] * index[None, :] % stations) * (2.0 * math.pi / stations)
    blocks = stations // BLADES
    shape = (blocks, BLADES, blocks, BLADES)
    return np.cos(angle).reshape(shape), np.sin(angle).reshape(shape)


def spread(block, row_span, row_at, col_span, col_at):
    count = block.shape[0]
    wide = np.zeros((count, row_span, count, col_span), np.float64)
    wide[:, row_at : row_at + BLADES, :, col_at : col_at + BLADES] = block
    return wide.reshape(count * row_span, count * col_span)


def rounded(values):
    return values.astype(np.float32).astype(ml_dtypes.bfloat16)


@functools.lru_cache(maxsize=None)
def forward_matrix(stations, span, at, split):
    pieces = []
    for part in phases(stations):
        exact = spread(part, ROWS, 0, span, at)
        head = rounded(exact)
        pieces.append(head)
        if split:
            pieces.append(rounded(exact - head.astype(np.float64)))
    return np.concatenate(pieces, axis=1)


@functools.lru_cache(maxsize=None)
def inverse_matrix(stations, span, at):
    return np.concatenate([rounded(spread(part, span, at, ROWS, 0)) for part in phases(stations)], axis=1)


def make_kernel(blocks, items, orders, width, split, spans, group):
    half = width // 2
    reach = orders // 2
    lines = round_up(ROWS * group, 16)
    norm = 1.0 / math.sqrt(blocks * BLADES)

    def body(gate_ref, data_ref, weight_ref, *rest):
        forward_refs = rest[:items]
        inverse_refs = rest[items : 2 * items]
        out_ref, modes_ref, moved_ref = rest[2 * items :]
        tail = None
        tail_at = 0
        for start in range(0, items, group):
            spectra = []
            for item in range(start, start + group):
                low, high, _ = spans[item]
                values = data_ref[:, low:high, :].reshape(blocks * (high - low), width)
                turned = jnp.concatenate([values[:, half:], -values[:, :half]], axis=1)
                stack = [values, values, turned, turned] if split else [values, turned]
                spectrum = jnp.dot(
                    forward_refs[item][...], jnp.concatenate(stack, axis=0), preferred_element_type=jnp.float32
                )
                spectra.append((spectrum * norm).reshape(blocks, ROWS, width))
            if lines > ROWS * group:
                spectra.append(jnp.zeros((blocks, lines - ROWS * group, width), jnp.float32))
            modes = jnp.concatenate(spectra, axis=1).astype(jnp.bfloat16)
            modes_ref[reach : reach + blocks] = modes
            modes_ref[:reach] = modes[blocks - reach :]
            modes_ref[reach + blocks :] = modes[:reach]
            for order in range(orders):
                for block in range(blocks):
                    piece = modes_ref[block + order]
                    keep = gate_ref[block, order] != 0
                    moved_ref[block, :, order * width : (order + 1) * width] = jnp.where(
                        keep, piece, jnp.zeros_like(piece)
                    )
            coupled = jnp.dot(
                moved_ref[...].reshape(blocks * lines, orders * width),
                weight_ref[...],
                preferred_element_type=jnp.float32,
            ).reshape(blocks, lines, width)
            for offset in range(group):
                item = start + offset
                low, high, _ = spans[item]
                own = coupled[:, offset * ROWS : (offset + 1) * ROWS].reshape(blocks * ROWS, width)
                own = own.astype(jnp.bfloat16)
                turned = jnp.concatenate([-own[:, half:], own[:, :half]], axis=1)
                result = jnp.dot(
                    inverse_refs[item][...],
                    jnp.concatenate([own, turned], axis=0),
                    preferred_element_type=jnp.float32,
                ).reshape(blocks, high - low, width)
                if tail is not None and tail_at == low:
                    joined = result[:, :8] + tail
                    result = jnp.concatenate([joined, result[:, 8:]], axis=1)
                last = item == items - 1 or spans[item + 1][0] >= high
                stop = high if last else spans[item + 1][0]
                out_ref[:, low:stop, :] = (result[:, : stop - low] * norm).astype(jnp.bfloat16)
                tail = None if last else result[:, stop - low :]
                tail_at = stop

    return body


def couple(gates, data, weights):
    blocks, lines, width = data.shape
    items = lines // BLADES
    orders = gates.shape[1]
    stations = blocks * BLADES
    spans = windows(items)
    group = 2 if items % 2 == 0 else 1
    split = True
    forward = [jnp.asarray(forward_matrix(stations, high - low, at, split)) for low, high, at in spans]
    inverse = [jnp.asarray(inverse_matrix(stations, high - low, at)) for low, high, at in spans]
    rows = round_up(ROWS * group, 16)
    in_vmem = pl.BlockSpec(memory_space=pltpu.VMEM)
    return pl.pallas_call(
        make_kernel(blocks, items, orders, width, split, spans, group),
        out_shape=jax.ShapeDtypeStruct(data.shape, jnp.bfloat16),
        in_specs=[pl.BlockSpec(memory_space=pltpu.SMEM)] + [in_vmem] * (2 + 2 * items),
        out_specs=in_vmem,
        scratch_shapes=[
            pltpu.VMEM((blocks + orders - 1, rows, width), jnp.bfloat16),
            pltpu.VMEM((blocks, rows, orders * width), jnp.bfloat16),
        ],
        compiler_params=pltpu.CompilerParams(vmem_limit_bytes=60 * 1024 * 1024),
        name="couple",
    )(gates, data, weights, *forward, *inverse)


def couple_plain(gates, data, weights):
    blocks, lines, width = data.shape
    half = width // 2
    orders = gates.shape[1]
    stations = blocks * BLADES
    norm = 1.0 / math.sqrt(stations)
    results = []
    for low, high, at in windows(lines // BLADES):
        values = data[:, low:high].reshape(blocks * (high - low), width)
        turned = jnp.concatenate([values[:, half:], -values[:, :half]], axis=1)
        spectrum = jnp.dot(
            jnp.asarray(forward_matrix(stations, high - low, at, True)),
            jnp.concatenate([values, values, turned, turned], axis=0),
            preferred_element_type=jnp.float32,
        )
        modes = (spectrum * norm).astype(jnp.bfloat16).reshape(blocks, ROWS, width)
        moved = [
            jnp.roll(modes, orders // 2 - order, axis=0) * gates[:, order].astype(jnp.bfloat16)[:, None, None]
            for order in range(orders)
        ]
        coupled = jnp.dot(
            jnp.concatenate(moved, axis=-1).reshape(blocks * ROWS, orders * width),
            weights,
            preferred_element_type=jnp.float32,
        ).astype(jnp.bfloat16)
        turned = jnp.concatenate([-coupled[:, half:], coupled[:, :half]], axis=1)
        result = jnp.dot(
            jnp.asarray(inverse_matrix(stations, high - low, at)),
            jnp.concatenate([coupled, turned], axis=0),
            preferred_element_type=jnp.float32,
        )
        own = (result * norm).astype(jnp.bfloat16).reshape(blocks, high - low, width)
        results.append(own[:, at : at + BLADES])
    joined = jnp.concatenate(results, axis=1)
    return jnp.pad(joined, ((0, 0), (0, lines - joined.shape[1]), (0, 0)))


def swap(values, axis):
    return lax.ppermute(values, axis, [(0, 1), (1, 0)])


def in_order(first, other, axis):
    mine_first = lax.axis_index(axis) == 0
    return jnp.stack([jnp.where(mine_first, first, other), jnp.where(mine_first, other, first)])


def shards(field, jacobian, coupling):
    local_stations, axial_count, freq_count, width = field.shape
    orders, _, _, own_rows, half = jacobian.shape
    peers = ("freq", "rest")
    rest = lax.axis_size("rest")
    groups = lax.axis_size("group")
    nodes = freq_count * rest
    items = axial_count // rest
    parts = groups * rest

    rows = jnp.concatenate([jacobian[:, :, 0], jacobian[:, :, 1]], axis=-1)
    if groups == 2 and rest == 2 and own_rows % parts == 0:
        piece = own_rows // parts
        rows = rows.reshape(orders, freq_count, groups, rest, piece, width).transpose(2, 1, 3, 0, 4, 5)
        mine = lax.dynamic_index_in_dim(rows, lax.axis_index("group"), 0, keepdims=False)
        mine = mine.reshape(nodes, orders * piece, width)
        got = lax.all_to_all(mine, peers, 0, 0, tiled=True)
    else:
        piece = None
        rows = rows.transpose(1, 0, 2, 3).reshape(freq_count, 1, orders * own_rows, width)
        rows = jnp.broadcast_to(rows, (freq_count, rest, orders * own_rows, width))
        got = lax.all_to_all(rows.reshape(nodes, orders * own_rows, width), peers, 0, 0, tiled=True)

    packed = field.reshape(local_stations, rest, items, freq_count, width).transpose(3, 1, 2, 0, 4)
    packed = packed.reshape(nodes, items * local_stations, width)
    lines = round_up(items * local_stations, 8)
    if lines != packed.shape[1]:
        packed = jnp.pad(packed, ((0, 0), (0, lines - packed.shape[1]), (0, 0)))
    got, packed = lax.optimization_barrier((got, packed))
    data = lax.all_to_all(packed, peers, 0, 0, tiled=True)

    if piece is not None:
        both = in_order(got, swap(got, "group"), "group")
        full = in_order(both, swap(both, "rest"), "rest")
        full = full.reshape(rest, groups, nodes, orders, piece, width).transpose(3, 2, 1, 0, 4, 5)
    else:
        full = got.reshape(nodes, orders, own_rows, width).transpose(1, 0, 2, 3)
    full = full.reshape(orders, nodes * own_rows, width)
    by_input = full.transpose(0, 2, 1)
    to_real = jnp.concatenate([by_input[:, :half], -by_input[:, half:]], axis=1)
    to_imag = jnp.concatenate([by_input[:, half:], by_input[:, :half]], axis=1)
    weights = jnp.concatenate([to_real, to_imag], axis=-1).reshape(orders * width, width)

    fits = nodes * local_stations <= 704
    result = (couple if fits else couple_plain)(coupling, data, weights)
    returned = lax.all_to_all(result, peers, 0, 0, tiled=True)[:, : items * local_stations]
    returned = returned.reshape(freq_count, rest, items, local_stations, width).transpose(3, 1, 2, 0, 4)
    return returned.reshape(local_stations, axial_count, freq_count, width)


def solution(mesh):
    names = tuple(mesh.axis_names)
    sizes = dict(mesh.shape)

    def whole(field, jacobian, coupling):
        freq_count = field.shape[2]
        devices = mesh.devices.reshape(sizes[names[0]], freq_count, sizes[names[1]] // freq_count)
        finer = Mesh(devices, ("group", "freq", "rest"))
        every = P(("group", "freq", "rest"), None, None, None)
        placed = (every, P(None, None, None, ("freq", "rest"), None), P())
        return jax.shard_map(shards, mesh=finer, in_specs=placed, out_specs=every, check_vma=False)(
            field, jacobian, coupling
        )

    return whole
```

time: 433 us -> 156 us (0.36)
  waiting for transfers between devices: 193 us -> 21.7 us
  blocking collectives: 84.3 us -> 50.4 us
  matrix products: 32.7 us -> 0 us
  other arithmetic: 41.7 us -> 10.6 us
  local copies, waits for them, and re-layouts: 61.2 us -> 32.7 us
  Pallas kernels: 0 us -> 25.1 us
    all_to_all x2, waiting for transfers between devices: 193 us -> 8.09 us  [the longest x1 8.09 us: shards(): got = lax.all_to_all(mine, peers, 0, 0, tiled=True)]
    all_to_all x1, blocking collectives: 84.3 us -> 50.4 us  [shards(): lax.all_to_all(result, peers, 0, 0, tiled=True)[:, :items * local_stations]]
    dot_general x52 -> x0, matrix products: 32.7 us -> none  [the longest x20 13.5 us: transform(): jnp.einsum('qri,oi->qro', moved, operator[order_idx], preferred_element_t...]
    pallas_call x0 -> x1, Pallas kernels: none -> 25.1 us  [couple(): pl.pallas_call(make_kernel(blocks, items, orders, width, split, spans, gr...]
    gather x1 -> x0, local copies, waits for them, and re-layouts: 21.1 us -> none  [shards(): outgoing = jnp.take(jacobian, jnp.asarray(targets, dtype=jnp.int32), axis=1)]
    concatenate x8 -> x1, other arithmetic: 25.2 us -> 7.41 us  [shards(): jnp.concatenate([to_real, to_imag], axis=-1).reshape(orders * width, width)]
    dynamic_slice x12 -> x0, local copies, waits for them, and re-layouts: 15.2 us -> none  [the longest x8 15 us: transform(): lax.dynamic_index_in_dim(local_jac, position, 1, keepdims=False)]
    reshape x1 -> x7, local copies, waits for them, and re-layouts: 1.44 us -> 16 us  [the longest x1 4.13 us: shards(): field.reshape(local_stations, rest, items, freq_count, width)]
  transfers between devices with their start and end apart: 2 -> 4, of which waited for: 2 -> 3; matrix products, arithmetic and copies ran while one was open for 5% -> 20% of each run, Pallas kernels for 0% -> 0%
where the time goes in v1:
time: 156 us; the launch traced here: 155 us
  blocking collectives  50.4 us (32%)
  local copies, waits for them, and re-layouts  32.7 us (21%)
  Pallas kernels  25.1 us (16%)
  waiting for transfers between devices  21.7 us (14%)
  starting transfers between devices  14.7 us (9%)
  other arithmetic  10.6 us (7%)
    all_to_all x1, blocking collectives, shards(): lax.all_to_all(result, peers, 0, 0, tiled=True)[:, :items * local_stations]  50.4 us
    pallas_call x1, Pallas kernels, couple(): pl.pallas_call(make_kernel(blocks, items, orders, width, split, spans, gr...  25.1 us
    ppermute x2, waiting for transfers between devices, swap(): return lax.ppermute(values, axis, [(0, 1), (1, 0)])  13.6 us
    all_to_all x1, waiting for transfers between devices, shards(): got = lax.all_to_all(mine, peers, 0, 0, tiled=True)  8.09 us
    concatenate x1, local copies, waits for them, and re-layouts, shards(): jnp.concatenate([to_real, to_imag], axis=-1).reshape(orders * width, width)  7.84 us
    concatenate x1, other arithmetic, shards(): jnp.concatenate([to_real, to_imag], axis=-1).reshape(orders * width, width)  7.41 us
    all_to_all x1, starting transfers between devices, shards(): got = lax.all_to_all(mine, peers, 0, 0, tiled=True)  7.35 us
    all_to_all x1, starting transfers between devices, shards(): data = lax.all_to_all(packed, peers, 0, 0, tiled=True)  5.11 us
  transfers between devices with their start and end apart: 4, of which 3 were waited for; matrix products, arithmetic and copies ran while one was open for 20% of the time, Pallas kernels for 0%

profile of v1, /device:TPU:1, one launch (start us, length us, event | category | flops | bytes accessed | tf_op | source)
XLA Modules:
  0.0 155.2 jit_solution(4410900254605500446)
XLA Ops:
  0.0 4.1 %fusion.2 = (bf16[5,8,1,20,320]{4,2,3,1,0:T(2,128)(2,1)S(1)}, bf16[5,8,1,20,320]{4,2,3,1,0:T(2,128)(2,1)S(1)}) fusion(bf16[5,8,2,20,320]{4,2,3,1,0:T(2,128)(2,1)} %param.12), kind=kLoop, calls=%fused_computation.14 | loop fusion | bytes 2048000 | tf_op jit(solution)/shard_map/slice | solution.py:214
  4.6 1.1 reshape.39
  5.6 7.3 %all-to-all-start = ((bf16[16,25,640]{2,1,0:T(8,128)(2,1)}), bf16[16,25,640]{2,1,0:T(8,128)(2,1)S(1)}, u32[]{:S(2)}, u32[]{:S(2)}) async-start(bf16[16,25,640]{2,1,0:T(8,128)(2,1)} %reshape.39), calls=%async_computation | async-start | bytes 1310720 | tf_op jit(solution)/shard_map/all_to_all | solution.py:220
  13.0 4.1 %copy.57 = bf16[22,2,4,8,640]{4,1,3,0,2:T(2,128)(2,1)} copy(bf16[22,2,4,8,640]{4,3,2,1,0:T(8,128)(2,1)} %bitcast.32) | data formatting | bytes 3604480 | tf_op jit(solution)/shard_map/reshape | solution.py:227
  17.1 4.0 %reshape.34 = bf16[16,88,640]{2,0,1:T(8,128)(2,1)S(1)} reshape(bf16[8,2,4,22,640]{4,1,0,3,2:T(2,128)(2,1)} %bitcast.27) | data formatting | bytes 3604480 | tf_op jit(solution)/shard_map/reshape | solution.py:228
  21.2 8.1 %all-to-all-done = bf16[16,25,640]{2,1,0:T(8,128)(2,1)S(1)} async-done(((bf16[16,25,640]{2,1,0:T(8,128)(2,1)}), bf16[16,25,640]{2,1,0:T(8,128)(2,1)S(1)}, u32[]{:S(2)}, u32[]{:S(2)}) %all-to-all-start) | async-done | bytes 512032 | tf_op jit(solution)/shard_map/all_to_all | solution.py:220
  29.2 1.6 %copy.39 = bf16[16,88,640]{2,1,0:T(8,128)(2,1)} copy(bf16[16,88,640]{2,0,1:T(8,128)(2,1)S(1)} %reshape.34) | data formatting | bytes 3604480 | tf_op jit(solution)/shard_map/optimization_barrier | solution.py:232
  30.8 5.1 %all-to-all-start.1 = ((bf16[16,88,640]{2,1,0:T(8,128)(2,1)}), bf16[16,88,640]{2,1,0:T(8,128)(2,1)}, u32[]{:S(2)}, u32[]{:S(2)}) async-start(bf16[16,88,640]{2,1,0:T(8,128)(2,1)} %copy.39), calls=%async_computation.1 | async-start | bytes 3604480 | tf_op jit(solution)/shard_map/all_to_all | solution.py:233
  36.1 1.3 collective-permute-start
  37.4 12.0 %collective-permute-done = bf16[16,25,640]{2,0,1:T(8,128)(2,1)S(1)} collective-permute-done((bf16[16,25,640]{2,0,1:T(8,128)(2,1)S(1)}, bf16[16,25,640]{2,0,1:T(8,128)(2,1)S(1)}, u32[]{:S(2)}, u32[]{:S(2)}) %collective-permute-start) | collective-permute-done | bytes 512032 | tf_op jit(solution)/shard_map/ppermute | solution.py:196
  49.7 0.9 collective-permute-start.1
  50.6 0.7 copy.45.gate_ref
  51.3 1.6 %collective-permute-done.1 = bf16[2,16,25,640]{3,1,2,0:T(8,128)(2,1)S(1)} collective-permute-done((bf16[2,16,25,640]{3,1,2,0:T(8,128)(2,1)S(1)}, bf16[2,16,25,640]{3,1,2,0:T(8,128)(2,1)S(1)}, u32[]{:S(2)}, u32[]{:S(2)}) %collective-permute-start.1) | collective-permute-done | bytes 1024032 | tf_op jit(solution)/shard_map/ppermute | solution.py:196
  52.9 0.2 broadcast_select_fusion.1
  53.3 0.7 copy.43
  54.0 2.8 %reshape.35 = bf16[5,320,640]{2,1,0:T(8,128)(2,1)} reshape(bf16[5,16,2,2,5,640]{5,4,3,2,1,0:T(8,128)(2,1)S(1)} %copy.43) | data formatting | bytes 4096000 | tf_op jit(solution)/shard_map/reshape | solution.py:241
  56.8 2.2 %slice_negate_fusion = (bf16[5,320,320]{1,2,0:T(8,128)(2,1)S(1)}, bf16[5,320,320]{1,2,0:T(8,128)(2,1)S(1)}, bf16[5,320,320]{1,2,0:T(8,128)(2,1)S(1)}) fusion(bf16[5,640,320]{1,2,0:T(8,128)(2,1)} %bitcast.25), kind=kLoop, calls=%fused_computation.13 | loop fusion | flops 512000 | bytes 5120000 | tf_op jit(solution)/shard_map/neg | solution.py:243
  59.0 7.4 %maximum_maximum_fusion = bf16[5,640,640]{1,2,0:T(8,128)(2,1)} fusion(bf16[5,320,320]{1,2,0:T(8,128)(2,1)S(1)} %get-tuple-element.11, bf16[5,320,320]{1,2,0:T(8,128)(2,1)S(1)} %get-tuple-element.10, bf16[5,320,320]{1,2,0:T(8,128)(2,1)S(1)} %get-tuple-element.9), kind=kLoop, calls=%fused_computation | loop fusion | flops 16384000 | bytes 7168000 | tf_op jit(solution)/shard_map/concatenate | solution.py:245
  66.4 7.8 %copy.44 = bf16[5,640,640]{2,1,0:T(8,128)(2,1)} copy(bf16[5,640,640]{1,2,0:T(8,128)(2,1)} %maximum_maximum_fusion) | data formatting | bytes 8192000 | tf_op jit(solution)/shard_map/concatenate | solution.py:245
  74.3 25.1 %couple.1 = bf16[16,88,640]{2,1,0:T(8,128)(2,1)} custom-call(s32[16,5]{1,0:T(8,128)} %copy.45.gate_ref, bf16[16,88,640]{2,1,0:T(8,128)(2,1)} %all-to-all-done.1.data_ref, bf16[3200,640]{1,0:T(8,128)(2,1)} %bitcast.24, bf16[384,1536]{1,0:T(8,128)(2,1)} %constant.31.clone.rest_0_, bf16[384,2048]{1,0:T(8,128)(2,1)} %constant.32.clone.rest_1_, ...), custom_call_target="tpu_custom_call" | custom-call | tf_op jit(solution)/shard_map/couple/pallas_call | solution.py:144
  99.4 50.4 %all_to_all.15 = bf16[16,88,640]{2,1,0:T(8,128)(2,1)} all-to-all(bf16[16,88,640]{2,1,0:T(8,128)(2,1)} %couple.1), channel_id=1, replica_groups=mesh['group'=2,'freq'=8,'rest'=2] {'freq','rest'}, dimensions={0} | all-to-all | bytes 3604480 | tf_op jit(solution)/shard_map/all_to_all | solution.py:249
  149.8 2.5 %reshape.40 = bf16[8,2,4,22,640]{4,3,2,1,0:T(8,128)(2,1)S(1)} reshape(bf16[16,88,640]{2,1,0:T(8,128)(2,1)} %all_to_all.15) | data formatting | bytes 3604480 | tf_op jit(solution)/shard_map/reshape | solution.py:250
  152.3 1.4 copy.56
  153.7 1.5 copy.47
  (11 shorter events, 1.2 us)
Async XLA Ops:
  5.6 23.6 %all-to-all-start = ((bf16[16,25,640]{2,1,0:T(8,128)(2,1)}), bf16[16,25,640]{2,1,0:T(8,128)(2,1)S(1)}, u32[]{:S(2)}, u32[]{:S(2)}) async-start(bf16[16,25,640]{2,1,0:T(8,128)(2,1)} %reshape.39), calls=%async_computation | async-start | bytes 1310720 | tf_op jit(solution)/shard_map/all_to_all | solution.py:220
  30.8 43.4 %all-to-all-start.1 = ((bf16[16,88,640]{2,1,0:T(8,128)(2,1)}), bf16[16,88,640]{2,1,0:T(8,128)(2,1)}, u32[]{:S(2)}, u32[]{:S(2)}) async-start(bf16[16,88,640]{2,1,0:T(8,128)(2,1)} %copy.39), calls=%async_computation.1 | async-start | bytes 3604480 | tf_op jit(solution)/shard_map/all_to_all | solution.py:233
  36.1 13.3 %collective-permute-start = (bf16[16,25,640]{2,0,1:T(8,128)(2,1)S(1)}, bf16[16,25,640]{2,0,1:T(8,128)(2,1)S(1)}, u32[]{:S(2)}, u32[]{:S(2)}) collective-permute-start(bf16[16,25,640]{2,0,1:T(8,128)(2,1)S(1)} %copy.41), channel_id=1, source_target_pairs={{0,16},{16,0},{1,17},{17,1},{2,18},{18,2},{3,19},{19,3},{4,20},{20... | collective-permute-start | bytes 1536008 | tf_op jit(solution)/shard_map/ppermute | solution.py:196
  37.4 13.3 %copy-start = (s32[16,5]{0,1:T(8,128)S(1)}, s32[16,5]{0,1:T(8,128)}, u32[]{:S(2)}) copy-start(s32[16,5]{0,1:T(8,128)} %param.13) | copy-start | bytes 964
  49.7 3.2 %collective-permute-start.1 = (bf16[2,16,25,640]{3,1,2,0:T(8,128)(2,1)S(1)}, bf16[2,16,25,640]{3,1,2,0:T(8,128)(2,1)S(1)}, u32[]{:S(2)}, u32[]{:S(2)}) collective-permute-start(bf16[2,16,25,640]{3,1,2,0:T(8,128)(2,1)S(1)} %pad_maximum_fusion), channel_id=1, source_target_pairs={{0,1},{1,0},{2,3},{3,2},{4,5},{5,4},{6,7},{7,6},{8,9},{9,8},{10,11... | collective-permute-start | bytes 3072008 | tf_op jit(solution)/shard_map/ppermute | solution.py:196

commit v2 on v1

--- a/solution.py
+++ b/solution.py
@@ -71,16 +71,28 @@
     lines = round_up(ROWS * group, 16)
     norm = 1.0 / math.sqrt(blocks * BLADES)
 
-    def body(gate_ref, data_ref, weight_ref, *rest):
-        forward_refs = rest[:items]
-        inverse_refs = rest[items : 2 * items]
-        out_ref, modes_ref, moved_ref = rest[2 * items :]
+    def body(gate_ref, *rest):
+        count = 2 + 2 * items
+        far, out_ref, near = rest[:count], rest[count], rest[count + 1 : 2 * count + 1]
+        modes_ref, moved_ref, sems = rest[2 * count + 1 :]
+        data_ref, weight_ref = near[0], near[1]
+        forward_refs, inverse_refs = near[2 : 2 + items], near[2 + items :]
+        copies = [pltpu.make_async_copy(far[index], near[index], sems.at[index]) for index in range(count)]
+        order_of_use = [0]
+        for start in range(0, items, group):
+            order_of_use += [2 + item for item in range(start, start + group)]
+            order_of_use += [1] if start == 0 else []
+            order_of_use += [2 + items + item for item in range(start, start + group)]
+        for index in order_of_use:
+            copies[index].start()
+        copies[0].wait()
         tail = None
         tail_at = 0
         for start in range(0, items, group):
             spectra = []
             for item in range(start, start + group):
                 low, high, _ = spans[item]
+                copies[2 + item].wait()
                 values = data_ref[:, low:high, :].reshape(blocks * (high - low), width)
                 turned = jnp.concatenate([values[:, half:], -values[:, :half]], axis=1)
                 stack = [values, values, turned, turned] if split else [values, turned]
@@ -101,6 +113,8 @@
                     moved_ref[block, :, order * width : (order + 1) * width] = jnp.where(
                         keep, piece, jnp.zeros_like(piece)
                     )
+            if start == 0:
+                copies[1].wait()
             coupled = jnp.dot(
                 moved_ref[...].reshape(blocks * lines, orders * width),
                 weight_ref[...],
@@ -111,6 +125,7 @@
                 low, high, _ = spans[item]
                 own = coupled[:, offset * ROWS : (offset + 1) * ROWS].reshape(blocks * ROWS, width)
                 own = own.astype(jnp.bfloat16)
+                copies[2 + items + item].wait()
                 turned = jnp.concatenate([-own[:, half:], own[:, :half]], axis=1)
                 result = jnp.dot(
                     inverse_refs[item][...],
@@ -140,19 +155,92 @@
     forward = [jnp.asarray(forward_matrix(stations, high - low, at, split)) for low, high, at in spans]
     inverse = [jnp.asarray(inverse_matrix(stations, high - low, at)) for low, high, at in spans]
     rows = round_up(ROWS * group, 16)
-    in_vmem = pl.BlockSpec(memory_space=pltpu.VMEM)
+    operands = [data, weights, *forward, *inverse]
     return pl.pallas_call(
         make_kernel(blocks, items, orders, width, split, spans, group),
         out_shape=jax.ShapeDtypeStruct(data.shape, jnp.bfloat16),
-        in_specs=[pl.BlockSpec(memory_space=pltpu.SMEM)] + [in_vmem] * (2 + 2 * items),
-        out_specs=in_vmem,
-        scratch_shapes=[
+        in_specs=[pl.BlockSpec(memory_space=pltpu.SMEM)] + [pl.BlockSpec(memory_space=pltpu.HBM)] * len(operands),
+        out_specs=pl.BlockSpec(memory_space=pltpu.VMEM),
+        scratch_shapes=[pltpu.VMEM(operand.shape, operand.dtype) for operand in operands]
+        + [
             pltpu.VMEM((blocks + orders - 1, rows, width), jnp.bfloat16),
             pltpu.VMEM((blocks, rows, orders * width), jnp.bfloat16),
+            pltpu.SemaphoreType.DMA((len(operands),)),
         ],
         compiler_params=pltpu.CompilerParams(vmem_limit_bytes=60 * 1024 * 1024),
         name="couple",
-    )(gates, data, weights, *forward, *inverse)
+    )(gates, *operands)
+
+
+@functools.lru_cache(maxsize=None)
+def reorder_matrix(stations, items, freqs):
+    rows = np.arange(stations * items * freqs).reshape(stations, items, freqs).transpose(2, 1, 0).reshape(-1)
+    return (rows[:, None] == np.arange(rows.size)[None, :]).astype(ml_dtypes.bfloat16)
+
+
+def reorder_body(matrix_ref, in_ref, out_ref):
+    width = in_ref.shape[-1]
+    moved = jnp.dot(matrix_ref[...], in_ref[...].reshape(-1, width), preferred_element_type=jnp.float32)
+    out_ref[...] = moved.astype(jnp.bfloat16).reshape(out_ref.shape)
+
+
+def pack(field, rest):
+    stations, axials, freqs, width = field.shape
+    items = axials // rest
+    matrix = jnp.asarray(reorder_matrix(stations, items, freqs))
+    return pl.pallas_call(
+        reorder_body,
+        grid=(rest,),
+        out_shape=jax.ShapeDtypeStruct((freqs, rest, items * stations, width), jnp.bfloat16),
+        in_specs=[
+            pl.BlockSpec(matrix.shape, lambda part: (0, 0)),
+            pl.BlockSpec((stations, items, freqs, width), lambda part: (0, part, 0, 0)),
+        ],
+        out_specs=pl.BlockSpec((freqs, 1, items * stations, width), lambda part: (0, part, 0, 0)),
+        compiler_params=pltpu.CompilerParams(vmem_limit_bytes=32 * 1024 * 1024),
+        name="pack",
+    )(matrix, field)
+
+
+def unpack(values, axials):
+    freqs, rest, lines, width = values.shape
+    items = axials // rest
+    stations = lines // items
+    matrix = jnp.asarray(reorder_matrix(stations, items, freqs).T)
+    return pl.pallas_call(
+        reorder_body,
+        grid=(rest,),
+        out_shape=jax.ShapeDtypeStruct((stations, axials, freqs, width), jnp.bfloat16),
+        in_specs=[
+            pl.BlockSpec(matrix.shape, lambda part: (0, 0)),
+            pl.BlockSpec((freqs, 1, lines, width), lambda part: (0, part, 0, 0)),
+        ],
+        out_specs=pl.BlockSpec((stations, items, freqs, width), lambda part: (0, part, 0, 0)),
+        compiler_params=pltpu.CompilerParams(vmem_limit_bytes=32 * 1024 * 1024),
+        name="unpack",
+    )(matrix, values)
+
+
+def real_form_body(in_ref, out_ref):
+    width = in_ref.shape[-1]
+    half = width // 2
+    by_input = in_ref[0].astype(jnp.float32).T
+    real, imag = by_input[:half], by_input[half:]
+    out_ref[:half] = jnp.concatenate([real, imag], axis=1).astype(jnp.bfloat16)
+    out_ref[half:] = jnp.concatenate([-imag, real], axis=1).astype(jnp.bfloat16)
+
+
+def real_form(full):
+    orders, half, width = full.shape
+    return pl.pallas_call(
+        real_form_body,
+        grid=(orders,),
+        out_shape=jax.ShapeDtypeStruct((orders * width, width), jnp.bfloat16),
+        in_specs=[pl.BlockSpec((1, half, width), lambda order: (order, 0, 0))],
+        out_specs=pl.BlockSpec((width, width), lambda order: (order, 0)),
+        compiler_params=pltpu.CompilerParams(vmem_limit_bytes=24 * 1024 * 1024),
+        name="real_form",
+    )(full)
 
 
 def couple_plain(gates, data, weights):
@@ -211,42 +299,54 @@
     items = axial_count // rest
     parts = groups * rest
 
-    rows = jnp.concatenate([jacobian[:, :, 0], jacobian[:, :, 1]], axis=-1)
-    if groups == 2 and rest == 2 and own_rows % parts == 0:
-        piece = own_rows // parts
-        rows = rows.reshape(orders, freq_count, groups, rest, piece, width).transpose(2, 1, 3, 0, 4, 5)
+    shared = groups == 2 and rest == 2 and own_rows % 2 == 0
+    if shared:
+        piece = own_rows // 2
+        rows = jacobian.reshape(orders, freq_count, 2, 2, piece, half).transpose(3, 1, 0, 4, 2, 5)
         mine = lax.dynamic_index_in_dim(rows, lax.axis_index("group"), 0, keepdims=False)
-        mine = mine.reshape(nodes, orders * piece, width)
-        got = lax.all_to_all(mine, peers, 0, 0, tiled=True)
+        chip = lax.axis_index("freq")
+        got = []
+        for step in range(freq_count):
+            block = lax.dynamic_index_in_dim(mine, chip ^ step, 0, keepdims=False)
+            pairs = [(index, index ^ step) for index in range(freq_count)]
+            got.append(lax.ppermute(block, "freq", pairs) if step else block)
     else:
-        piece = None
+        rows = jnp.concatenate([jacobian[:, :, 0], jacobian[:, :, 1]], axis=-1)
         rows = rows.transpose(1, 0, 2, 3).reshape(freq_count, 1, orders * own_rows, width)
         rows = jnp.broadcast_to(rows, (freq_count, rest, orders * own_rows, width))
         got = lax.all_to_all(rows.reshape(nodes, orders * own_rows, width), peers, 0, 0, tiled=True)
 
-    packed = field.reshape(local_stations, rest, items, freq_count, width).transpose(3, 1, 2, 0, 4)
-    packed = packed.reshape(nodes, items * local_stations, width)
+    fits = nodes * local_stations <= 704 and items * local_stations % 8 == 0
+    if fits:
+        packed = pack(field, rest).reshape(nodes, items * local_stations, width)
+    else:
+        packed = field.reshape(local_stations, rest, items, freq_count, width).transpose(3, 1, 2, 0, 4)
+        packed = packed.reshape(nodes, items * local_stations, width)
     lines = round_up(items * local_stations, 8)
     if lines != packed.shape[1]:
         packed = jnp.pad(packed, ((0, 0), (0, lines - packed.shape[1]), (0, 0)))
     got, packed = lax.optimization_barrier((got, packed))
     data = lax.all_to_all(packed, peers, 0, 0, tiled=True)
 
-    if piece is not None:
-        both = in_order(got, swap(got, "group"), "group")
+    if shared:
+        ordered = jnp.stack(got)
+        for bit in range(freq_count.bit_length() - 1):
+            halves = ordered.reshape((freq_count >> (bit + 1), 2, 1 << bit) + ordered.shape[1:])
+            flipped = jnp.where((chip >> bit) & 1 == 1, halves[:, ::-1], halves)
+            ordered = flipped.reshape(ordered.shape)
+        both = in_order(ordered, swap(ordered, "group"), "group")
         full = in_order(both, swap(both, "rest"), "rest")
-        full = full.reshape(rest, groups, nodes, orders, piece, width).transpose(3, 2, 1, 0, 4, 5)
+        full = full.transpose(3, 2, 0, 1, 4, 5, 6)
     else:
         full = got.reshape(nodes, orders, own_rows, width).transpose(1, 0, 2, 3)
     full = full.reshape(orders, nodes * own_rows, width)
-    by_input = full.transpose(0, 2, 1)
-    to_real = jnp.concatenate([by_input[:, :half], -by_input[:, half:]], axis=1)
-    to_imag = jnp.concatenate([by_input[:, half:], by_input[:, :half]], axis=1)
-    weights = jnp.concatenate([to_real, to_imag], axis=-1).reshape(orders * width, width)
-
-    fits = nodes * local_stations <= 704
+    weights = real_form(full)
+
     result = (couple if fits else couple_plain)(coupling, data, weights)
-    returned = lax.all_to_all(result, peers, 0, 0, tiled=True)[:, : items * local_stations]
+    returned = lax.all_to_all(result, peers, 0, 0, tiled=True)
+    if fits:
+        return unpack(returned.reshape(freq_count, rest, items * local_stations, width), axial_count)
+    returned = returned[:, : items * local_stations]
     returned = returned.reshape(freq_count, rest, items, local_stations, width).transpose(3, 1, 2, 0, 4)
     return returned.reshape(local_stations, axial_count, freq_count, width)
 

time: 156 us -> 148 us (0.949)
  local copies, waits for them, and re-layouts: 32.7 us -> 11.7 us
  Pallas kernels: 25.1 us -> 34.4 us
  starting transfers between devices: 14.7 us -> 20.6 us
  waiting for transfers between devices: 21.7 us -> 18.8 us
  other arithmetic: 10.6 us -> 13 us
  blocking collectives: 50.4 us -> 48.7 us
    reshape x6 -> x0, local copies, waits for them, and re-layouts: 13.2 us -> none  [the longest x1 4.13 us: shards(): field.reshape(local_stations, rest, items, freq_count, width)]
    ppermute x0 -> x7, starting transfers between devices: none -> 10.2 us  [shards(): got.append(lax.ppermute(block, 'freq', pairs) if step else block)]
    pallas_call x0 -> x3, Pallas kernels: none -> 8.49 us  [the longest x1 3.12 us: unpack(): pl.pallas_call(reorder_body, grid=(rest,), out_shape=jax.ShapeDtypeStruct...]
    all_to_all x1 -> x0, waiting for transfers between devices: 8.09 us -> none  [shards(): got = lax.all_to_all(mine, peers, 0, 0, tiled=True)]
    concatenate x1 -> x0, local copies, waits for them, and re-layouts: 7.84 us -> none  [shards(): jnp.concatenate([to_real, to_imag], axis=-1).reshape(orders * width, width)]
    concatenate x1 -> x0, other arithmetic: 7.41 us -> none  [shards(): jnp.concatenate([to_real, to_imag], axis=-1).reshape(orders * width, width)]
    all_to_all x1 -> x0, starting transfers between devices: 7.35 us -> none  [shards(): got = lax.all_to_all(mine, peers, 0, 0, tiled=True)]
    another operation x2 -> x3, other arithmetic: 0.31 us -> 6.66 us  [in_order(): jnp.stack([jnp.where(mine_first, first, other), jnp.where(mine_first, oth...]
  transfers between devices with their start and end apart: 4 -> 10, of which waited for: 3 -> 3; matrix products, arithmetic and copies ran while one was open for 20% -> 12% of each run, Pallas kernels for 0% -> 4%
where the time goes in v2:
time: 148 us; the launch traced here: 147 us
  blocking collectives  48.7 us (33%)
  Pallas kernels  34.4 us (23%)
  starting transfers between devices  20.6 us (14%)
  waiting for transfers between devices  18.8 us (13%)
  other arithmetic  13 us (9%)
  local copies, waits for them, and re-layouts  11.7 us (8%)
    all_to_all x1, blocking collectives, shards(): returned = lax.all_to_all(result, peers, 0, 0, tiled=True)  48.7 us
    pallas_call x1, Pallas kernels, couple(): pl.pallas_call(make_kernel(blocks, items, orders, width, split, spans, gr...  25.9 us
    ppermute x2, waiting for transfers between devices, swap(): return lax.ppermute(values, axis, [(0, 1), (1, 0)])  16.3 us
    ppermute x7, starting transfers between devices, shards(): got.append(lax.ppermute(block, 'freq', pairs) if step else block)  10.2 us
    all_to_all x1, starting transfers between devices, shards(): data = lax.all_to_all(packed, peers, 0, 0, tiled=True)  8.26 us
    another operation x3, other arithmetic, in_order(): jnp.stack([jnp.where(mine_first, first, other), jnp.where(mine_first, oth...  6.66 us
    reshape x1, local copies, waits for them, and re-layouts, shards(): full = full.reshape(orders, nodes * own_rows, width)  5 us
    transpose x1, other arithmetic, shards(): full = full.transpose(3, 2, 0, 1, 4, 5, 6)  4.93 us
  transfers between devices with their start and end apart: 10, of which 3 were waited for; matrix products, arithmetic and copies ran while one was open for 12% of the time, Pallas kernels for 4%

profile of v2, /device:TPU:1, one launch (start us, length us, event | category | flops | bytes accessed | tf_op | source)
XLA Modules:
  0.0 147.4 jit_solution(6214543709291071422)
XLA Ops:
  0.0 1.7 %dynamic-slice_bitcast_fusion = (bf16[5,10,2,320]{3,2,1,0:T(2,128)(2,1)S(1)}, bf16[5,10,2,320]{3,2,1,0:T(2,128)(2,1)S(1)}, bf16[5,10,2,320]{3,2,1,0:T(2,128)(2,1...) fusion(bf16[5,8,2,2,10,320]{5,2,4,3,1,0:T(2,128)(2,1)} %bitcast, ...), kind=kLoop, calls=%fused_computation.21 | loop fusion | bytes 1024036 | tf_op jit(solution)/shard_map/jit(dynamic_index_in_dim)/squeeze | solution.py:310
  1.7 2.1 %collective-permute-start = (bf16[5,10,2,320]{3,2,1,0:T(2,128)(2,1)S(1)}, bf16[5,10,2,320]{3,2,1,0:T(2,128)(2,1)S(1)}, u32[]{:S(2)}, u32[]{:S(2)}) collective-permute-start(bf16[5,10,2,320]{3,2,1,0:T(2,128)(2,1)S(1)} %get-tuple-element.32), channel_id=1, source_target_pairs={{0,2},{2,0},{4,6},{6,4},{8,10},{10,8},{12,14},{14,12},{1,3},{3,1},... | collective-permute-start | bytes 192008 | tf_op jit(solution)/shard_map/ppermute | solution.py:312
  3.8 1.3 collective-permute-start.1
  5.1 2.4 %collective-permute-start.3 = (bf16[5,10,2,320]{3,2,1,0:T(2,128)(2,1)S(1)}, bf16[5,10,2,320]{3,2,1,0:T(2,128)(2,1)S(1)}, u32[]{:S(2)}, u32[]{:S(2)}) collective-permute-start(bf16[5,10,2,320]{3,2,1,0:T(2,128)(2,1)S(1)} %get-tuple-element.29), channel_id=1, source_target_pairs={{0,8},{2,10},{4,12},{6,14},{8,0},{10,2},{12,4},{14,6},{1,9},{3,11}... | collective-permute-start | bytes 192008 | tf_op jit(solution)/shard_map/ppermute | solution.py:312
  7.5 1.0 collective-permute-start.4
  8.5 3.3 %collective-permute-start.5 = (bf16[5,10,2,320]{3,2,1,0:T(2,128)(2,1)S(1)}, bf16[5,10,2,320]{3,2,1,0:T(2,128)(2,1)S(1)}, u32[]{:S(2)}, u32[]{:S(2)}) collective-permute-start(bf16[5,10,2,320]{3,2,1,0:T(2,128)(2,1)S(1)} %get-tuple-element.34), channel_id=1, source_target_pairs={{0,12},{2,14},{4,8},{6,10},{8,4},{10,6},{12,0},{14,2},{1,13},{3,15... | collective-permute-start | bytes 192008 | tf_op jit(solution)/shard_map/ppermute | solution.py:312
  11.9 1.5 %copy-done.1 = bf16[22,8,8,640]{3,2,1,0:T(8,128)(2,1)S(1)} copy-done((bf16[22,8,8,640]{3,2,1,0:T(8,128)(2,1)S(1)}, bf16[22,8,8,640]{3,2,1,0:T(8,128)(2,1)}, u32[]{:S(2)}) %copy-start.1) | copy-done | bytes 1802264
  13.4 3.1 %pack.1 = bf16[8,2,88,640]{3,2,1,0:T(8,128)(2,1)} custom-call(bf16[704,704]{1,0:T(8,128)(2,1)S(1)} %copy-done.3, bf16[22,8,8,640]{3,2,1,0:T(8,128)(2,1)S(1)} %copy-done.1), custom_call_target="tpu_custom_call" | custom-call | tf_op jit(solution)/shard_map/pack/pallas_call | solution.py:191
  16.5 2.5 %collective-permute-done.4 = bf16[5,10,2,320]{3,2,1,0:T(2,128)(2,1)S(1)} collective-permute-done((bf16[5,10,2,320]{3,2,1,0:T(2,128)(2,1)S(1)}, bf16[5,10,2,320]{3,2,1,0:T(2,128)(2,1)S(1)}, u32[]{:S(2)}, u32[]{:S(2)}) %collective-permute-start.4) | collective-permute-done | bytes 64032 | tf_op jit(solution)/shard_map/ppermute | solution.py:312
  20.5 8.3 %all-to-all-start = ((bf16[16,88,640]{2,1,0:T(8,128)(2,1)}), bf16[16,88,640]{2,1,0:T(8,128)(2,1)}, u32[]{:S(2)}, u32[]{:S(2)}) async-start(bf16[16,88,640]{2,1,0:T(8,128)(2,1)} %bitcast.17), calls=%async_computation | async-start | bytes 3604480 | tf_op jit(solution)/shard_map/all_to_all | solution.py:329
  29.8 1.3 collective-permute-start.7
  31.0 14.2 %collective-permute-done.7 = bf16[8,5,10,2,320]{4,3,2,0,1:T(2,128)(2,1)S(1)} collective-permute-done((bf16[8,5,10,2,320]{4,3,2,0,1:T(2,128)(2,1)S(1)}, bf16[8,5,10,2,320]{4,3,2,0,1:T(2,128)(2,1)S(1)}, u32[]{:S(2)}, u32[]{:S(2)}) %collective-permute-start.7) | collective-permute-done | bytes 512032 | tf_op jit(solution)/shard_map/ppermute | solution.py:284
  45.2 1.0 fusion.2
  46.2 2.8 %pad_maximum_fusion = bf16[2,8,5,10,2,320]{5,4,3,0,1,2:T(2,128)(2,1)} fusion(bf16[1,8,5,10,2,320]{5,4,3,0,1,2:T(2,128)(2,1)S(1)} %get-tuple-element.26, bf16[1,8,5,10,2,320]{5,4,3,0,1,2:T(2,128)(2,1)S(1)} %get-tuple-element.25), kind=kLoop, calls=%fused_computation.5 | loop fusion | flops 512000 | bytes 2048000 | tf_op jit(solution)/shard_map/stack | solution.py:289
  49.0 0.9 collective-permute-start.8
  50.5 2.1 %collective-permute-done.8 = bf16[2,8,5,10,2,320]{5,4,3,0,1,2:T(2,128)(2,1)S(1)} collective-permute-done((bf16[2,8,5,10,2,320]{5,4,3,0,1,2:T(2,128)(2,1)}, bf16[2,8,5,10,2,320]{5,4,3,0,1,2:T(2,128)(2,1)S(1)}, u32[]{:S(2)}, u32[]{:S(2)}) %collective-permute-start.8) | collective-permute-done | bytes 1024032 | tf_op jit(solution)/shard_map/ppermute | solution.py:284
  52.6 2.9 %fusion = (bf16[1,2,8,5,10,2,320]{6,5,4,1,0,2,3:T(2,128)(2,1)S(1)}, bf16[1,2,8,5,10,2,320]{6,5,4,1,0,2,3:T(2,128)(2,1)S(1)}) fusion(bf16[2,8,5,10,2,320]{5,4,3,0,1,2:T(2,128)(2,1)S(1)} %collective-permute-done.8, pred[]{:T(512)S(6)} %eq.15, bf16[1,8,5,10,2,320]{5,4,3,0,1,2:T(2,128)(2,1)S(1)} %get-tuple-element.26, ...), kind=kLoop, calls=%fused_computation.3 | loop fusion | flops 1536000 | bytes 4096001 | tf_op jit(solution)/shard_map/stack | solution.py:289
  55.5 4.9 %maximum_bitcast_fusion = bf16[5,8,2,2,10,2,320]{6,5,4,3,2,1,0:T(2,128)(2,1)} fusion(bf16[1,2,8,5,10,2,320]{6,5,4,1,0,2,3:T(2,128)(2,1)S(1)} %get-tuple-element.24, bf16[1,2,8,5,10,2,320]{6,5,4,1,0,2,3:T(2,128)(2,1)S(1)} %get-tuple-element.23), kind=kLoop, calls=%fused_computation | loop fusion | flops 1024000 | bytes 4096000 | tf_op jit(solution)/shard_map/transpose | solution.py:339
  60.5 5.0 %reshape.38.in_ref = bf16[5,320,640]{2,1,0:T(8,128)(2,1)S(1)} reshape(bf16[5,8,2,2,10,2,320]{6,5,4,3,2,1,0:T(2,128)(2,1)} %maximum_bitcast_fusion) | data formatting | bytes 4096000 | tf_op jit(solution)/shard_map/reshape | solution.py:342
  65.5 2.2 %real_form.1.rest_1_ = bf16[3200,640]{1,0:T(8,128)(2,1)S(1)} custom-call(bf16[5,320,640]{2,1,0:T(8,128)(2,1)S(1)} %reshape.38.in_ref), custom_call_target="tpu_custom_call" | custom-call | tf_op jit(solution)/shard_map/real_form/pallas_call | solution.py:235
  67.7 1.9 %copy-done = bf16[3200,640]{1,0:T(8,128)(2,1)} copy-done((bf16[3200,640]{1,0:T(8,128)(2,1)}, bf16[3200,640]{1,0:T(8,128)(2,1)S(1)}, u32[]{:S(2)}) %copy-start) | copy-done | bytes 4096024
  69.7 25.9 %couple.1 = bf16[16,88,640]{2,1,0:T(8,128)(2,1)} custom-call(s32[16,5]{1,0:T(8,128)} %copy.25.gate_ref, bf16[16,88,640]{2,1,0:T(8,128)(2,1)} %all-to-all-done.rest_0_, bf16[3200,640]{1,0:T(8,128)(2,1)} %copy-done, bf16[384,1536]{1,0:T(8,128)(2,1)} %constant.296.clone.rest_2_, bf16[384,2048]{1,0:T(8,128)(2,1)} %constant.297.clone.rest_3_, ...), custom_call_target="tpu_custom_call" | custom-call | tf_op jit(solution)/shard_map/couple/pallas_call | solution.py:159
  95.5 48.7 %all_to_all.10 = bf16[16,88,640]{2,1,0:T(8,128)(2,1)S(1)} all-to-all(bf16[16,88,640]{2,1,0:T(8,128)(2,1)} %couple.1), channel_id=1, replica_groups=mesh['group'=2,'freq'=8,'rest'=2] {'freq','rest'}, dimensions={0} | all-to-all | bytes 3604480 | tf_op jit(solution)/shard_map/all_to_all | solution.py:346
  144.2 3.1 %unpack.1 = bf16[22,8,8,640]{3,2,1,0:T(8,128)(2,1)} custom-call(bf16[704,704]{1,0:T(8,128)(2,1)S(1)} %copy-done.2, bf16[8,2,88,640]{3,2,1,0:T(8,128)(2,1)S(1)} %bitcast.83), custom_call_target="tpu_custom_call" | custom-call | tf_op jit(solution)/shard_map/unpack/pallas_call | solution.py:210
  (30 shorter events, 3.2 us)
Async XLA Ops:
  0.0 11.9 %copy-start.3 = (bf16[704,704]{1,0:T(8,128)(2,1)S(1)}, bf16[704,704]{1,0:T(8,128)(2,1)}, u32[]{:S(2)}) copy-start(bf16[704,704]{1,0:T(8,128)(2,1)} %constant.295.clone.matrix_ref) | copy-start | bytes 2973700
  1.7 6.9 %collective-permute-start = (bf16[5,10,2,320]{3,2,1,0:T(2,128)(2,1)S(1)}, bf16[5,10,2,320]{3,2,1,0:T(2,128)(2,1)S(1)}, u32[]{:S(2)}, u32[]{:S(2)}) collective-permute-start(bf16[5,10,2,320]{3,2,1,0:T(2,128)(2,1)S(1)} %get-tuple-element.32), channel_id=1, source_target_pairs={{0,2},{2,0},{4,6},{6,4},{8,10},{10,8},{12,14},{14,12},{1,3},{3,1},... | collective-permute-start | bytes 192008 | tf_op jit(solution)/shard_map/ppermute | solution.py:312
  3.8 8.1 %collective-permute-start.1 = (bf16[5,10,2,320]{3,2,1,0:T(2,128)(2,1)S(1)}, bf16[5,10,2,320]{3,2,1,0:T(2,128)(2,1)S(1)}, u32[]{:S(2)}, u32[]{:S(2)}) collective-permute-start(bf16[5,10,2,320]{3,2,1,0:T(2,128)(2,1)S(1)} %get-tuple-element.31), channel_id=1, source_target_pairs={{0,4},{2,6},{4,0},{6,2},{8,12},{10,14},{12,8},{14,10},{1,5},{3,7},... | collective-permute-start | bytes 192008 | tf_op jit(solution)/shard_map/ppermute | solution.py:312
  5.1 11.4 %collective-permute-start.2 = (bf16[5,10,2,320]{3,2,1,0:T(2,128)(2,1)S(1)}, bf16[5,10,2,320]{3,2,1,0:T(2,128)(2,1)S(1)}, u32[]{:S(2)}, u32[]{:S(2)}) collective-permute-start(bf16[5,10,2,320]{3,2,1,0:T(2,128)(2,1)S(1)} %get-tuple-element.30), channel_id=1, source_target_pairs={{0,6},{2,4},{4,2},{6,0},{8,14},{10,12},{12,10},{14,8},{1,7},{3,5},... | collective-permute-start | bytes 192008 | tf_op jit(solution)/shard_map/ppermute | solution.py:312
  5.1 11.4 %collective-permute-start.3 = (bf16[5,10,2,320]{3,2,1,0:T(2,128)(2,1)S(1)}, bf16[5,10,2,320]{3,2,1,0:T(2,128)(2,1)S(1)}, u32[]{:S(2)}, u32[]{:S(2)}) collective-permute-start(bf16[5,10,2,320]{3,2,1,0:T(2,128)(2,1)S(1)} %get-tuple-element.29), channel_id=1, source_target_pairs={{0,8},{2,10},{4,12},{6,14},{8,0},{10,2},{12,4},{14,6},{1,9},{3,11}... | collective-permute-start | bytes 192008 | tf_op jit(solution)/shard_map/ppermute | solution.py:312
  7.5 11.5 %collective-permute-start.4 = (bf16[5,10,2,320]{3,2,1,0:T(2,128)(2,1)S(1)}, bf16[5,10,2,320]{3,2,1,0:T(2,128)(2,1)S(1)}, u32[]{:S(2)}, u32[]{:S(2)}) collective-permute-start(bf16[5,10,2,320]{3,2,1,0:T(2,128)(2,1)S(1)} %get-tuple-element.28), channel_id=1, source_target_pairs={{0,10},{2,8},{4,14},{6,12},{8,2},{10,0},{12,6},{14,4},{1,11},{3,9}... | collective-permute-start | bytes 192008 | tf_op jit(solution)/shard_map/ppermute | solution.py:312
  8.5 10.4 %collective-permute-start.5 = (bf16[5,10,2,320]{3,2,1,0:T(2,128)(2,1)S(1)}, bf16[5,10,2,320]{3,2,1,0:T(2,128)(2,1)S(1)}, u32[]{:S(2)}, u32[]{:S(2)}) collective-permute-start(bf16[5,10,2,320]{3,2,1,0:T(2,128)(2,1)S(1)} %get-tuple-element.34), channel_id=1, source_target_pairs={{0,12},{2,14},{4,8},{6,10},{8,4},{10,6},{12,0},{14,2},{1,13},{3,15... | collective-permute-start | bytes 192008 | tf_op jit(solution)/shard_map/ppermute | solution.py:312
  11.9 7.1 %collective-permute-start.6 = (bf16[5,10,2,320]{3,2,1,0:T(2,128)(2,1)S(1)}, bf16[5,10,2,320]{3,2,1,0:T(2,128)(2,1)S(1)}, u32[]{:S(2)}, u32[]{:S(2)}) collective-permute-start(bf16[5,10,2,320]{3,2,1,0:T(2,128)(2,1)S(1)} %get-tuple-element.27), channel_id=1, source_target_pairs={{0,14},{2,12},{4,10},{6,8},{8,6},{10,4},{12,2},{14,0},{1,15},{3,13... | collective-permute-start | bytes 192008 | tf_op jit(solution)/shard_map/ppermute | solution.py:312
  11.9 1.5 %copy-start.1 = (bf16[22,8,8,640]{3,2,1,0:T(8,128)(2,1)S(1)}, bf16[22,8,8,640]{3,2,1,0:T(8,128)(2,1)}, u32[]{:S(2)}) copy-start(bf16[22,8,8,640]{3,2,1,0:T(8,128)(2,1)} %in_ref.1) | copy-start | bytes 5406724
  20.5 49.1 %all-to-all-start = ((bf16[16,88,640]{2,1,0:T(8,128)(2,1)}), bf16[16,88,640]{2,1,0:T(8,128)(2,1)}, u32[]{:S(2)}, u32[]{:S(2)}) async-start(bf16[16,88,640]{2,1,0:T(8,128)(2,1)} %bitcast.17), calls=%async_computation | async-start | bytes 3604480 | tf_op jit(solution)/shard_map/all_to_all | solution.py:329
  29.8 15.5 %collective-permute-start.7 = (bf16[8,5,10,2,320]{4,3,2,0,1:T(2,128)(2,1)S(1)}, bf16[8,5,10,2,320]{4,3,2,0,1:T(2,128)(2,1)S(1)}, u32[]{:S(2)}, u32[]{:S(2)}) collective-permute-start(bf16[8,5,10,2,320]{4,3,2,0,1:T(2,128)(2,1)S(1)} %bitcast.84), channel_id=1, source_target_pairs={{0,16},{16,0},{1,17},{17,1},{2,18},{18,2},{3,19},{19,3},{4,20},{20... | collective-permute-start | bytes 1536008 | tf_op jit(solution)/shard_map/ppermute | solution.py:284
  46.2 3.6 %copy-start.4 = (s32[16,5]{0,1:T(8,128)S(1)}, s32[16,5]{0,1:T(8,128)}, u32[]{:S(2)}) copy-start(s32[16,5]{0,1:T(8,128)} %param.15) | copy-start | bytes 964
  49.0 3.6 %collective-permute-start.8 = (bf16[2,8,5,10,2,320]{5,4,3,0,1,2:T(2,128)(2,1)}, bf16[2,8,5,10,2,320]{5,4,3,0,1,2:T(2,128)(2,1)S(1)}, u32[]{:S(2)}, u32[]{:S(2)}) collective-permute-start(bf16[2,8,5,10,2,320]{5,4,3,0,1,2:T(2,128)(2,1)} %pad_maximum_fusion), channel_id=1, source_target_pairs={{0,1},{1,0},{2,3},{3,2},{4,5},{5,4},{6,7},{7,6},{8,9},{9,8},{10,11... | collective-permute-start | bytes 3072008 | tf_op jit(solution)/shard_map/ppermute | solution.py:284
  67.7 1.9 %copy-start = (bf16[3200,640]{1,0:T(8,128)(2,1)}, bf16[3200,640]{1,0:T(8,128)(2,1)S(1)}, u32[]{:S(2)}) copy-start(bf16[3200,640]{1,0:T(8,128)(2,1)S(1)} %real_form.1.rest_1_) | copy-start | bytes 12288004
  95.5 48.7 %copy-start.2 = (bf16[704,704]{1,0:T(8,128)(2,1)S(1)}, bf16[704,704]{1,0:T(8,128)(2,1)}, u32[]{:S(2)}) copy-start(bf16[704,704]{1,0:T(8,128)(2,1)} %constant.304.clone.matrix_ref) | copy-start | bytes 2973700

commit v3 on v2

--- a/solution.py
+++ b/solution.py
@@ -63,6 +63,14 @@
 @functools.lru_cache(maxsize=None)
 def inverse_matrix(stations, span, at):
     return np.concatenate([rounded(spread(part, span, at, ROWS, 0)) for part in phases(stations)], axis=1)
+
+
+def product(read, right, count, pieces):
+    size = count // pieces
+    parts = [
+        jnp.dot(read(piece * size, size), right, preferred_element_type=jnp.float32) for piece in range(pieces)
+    ]
+    return jnp.concatenate(parts, axis=0)
 
 
 def make_kernel(blocks, items, orders, width, split, spans, group):
@@ -96,8 +104,12 @@
                 values = data_ref[:, low:high, :].reshape(blocks * (high - low), width)
                 turned = jnp.concatenate([values[:, half:], -values[:, :half]], axis=1)
                 stack = [values, values, turned, turned] if split else [values, turned]
-                spectrum = jnp.dot(
-                    forward_refs[item][...], jnp.concatenate(stack, axis=0), preferred_element_type=jnp.float32
+                forward_ref = forward_refs[item]
+                spectrum = product(
+                    lambda first, size, ref=forward_ref: ref[first : first + size],
+                    jnp.concatenate(stack, axis=0),
+                    blocks * ROWS,
+                    2,
                 )
                 spectra.append((spectrum * norm).reshape(blocks, ROWS, width))
             if lines > ROWS * group:
@@ -115,10 +127,11 @@
                     )
             if start == 0:
                 copies[1].wait()
-            coupled = jnp.dot(
-                moved_ref[...].reshape(blocks * lines, orders * width),
+            coupled = product(
+                lambda first, size: moved_ref[first : first + size].reshape(size * lines, orders * width),
                 weight_ref[...],
-                preferred_element_type=jnp.float32,
+                blocks,
+                4,
             ).reshape(blocks, lines, width)
             for offset in range(group):
                 item = start + offset
@@ -127,10 +140,12 @@
                 own = own.astype(jnp.bfloat16)
                 copies[2 + items + item].wait()
                 turned = jnp.concatenate([-own[:, half:], own[:, :half]], axis=1)
-                result = jnp.dot(
-                    inverse_refs[item][...],
+                inverse_ref = inverse_refs[item]
+                result = product(
+                    lambda first, size, ref=inverse_ref: ref[first : first + size],
                     jnp.concatenate([own, turned], axis=0),
-                    preferred_element_type=jnp.float32,
+                    blocks * (high - low),
+                    2,
                 ).reshape(blocks, high - low, width)
                 if tail is not None and tail_at == low:
                     joined = result[:, :8] + tail

time: 148 us -> 143 us (0.966)
  Pallas kernels: 34.4 us -> 29.4 us
    pallas_call x1, Pallas kernels: 25.9 us -> 20.9 us  [couple(): pl.pallas_call(make_kernel(blocks, items, orders, width, split, spans, gr...]
  transfers between devices with their start and end apart: 10 -> 10, of which waited for: 3 -> 3; matrix products, arithmetic and copies ran while one was open for 12% -> 13% of each run, Pallas kernels for 4% -> 4%
where the time goes in v3:
time: 143 us; the launch traced here: 142 us
  blocking collectives  48.7 us (34%)
  Pallas kernels  29.4 us (21%)
  starting transfers between devices  20.6 us (14%)
  waiting for transfers between devices  18.8 us (13%)
  other arithmetic  13 us (9%)
  local copies, waits for them, and re-layouts  11.7 us (8%)
    all_to_all x1, blocking collectives, shards(): returned = lax.all_to_all(result, peers, 0, 0, tiled=True)  48.7 us
    pallas_call x1, Pallas kernels, couple(): pl.pallas_call(make_kernel(blocks, items, orders, width, split, spans, gr...  20.9 us
    ppermute x2, waiting for transfers between devices, swap(): return lax.ppermute(values, axis, [(0, 1), (1, 0)])  16.3 us
    ppermute x7, starting transfers between devices, shards(): got.append(lax.ppermute(block, 'freq', pairs) if step else block)  10.2 us
    all_to_all x1, starting transfers between devices, shards(): data = lax.all_to_all(packed, peers, 0, 0, tiled=True)  8.26 us
    another operation x3, other arithmetic, in_order(): jnp.stack([jnp.where(mine_first, first, other), jnp.where(mine_first, oth...  6.66 us
    reshape x1, local copies, waits for them, and re-layouts, shards(): full = full.reshape(orders, nodes * own_rows, width)  5 us
    transpose x1, other arithmetic, shards(): full = full.transpose(3, 2, 0, 1, 4, 5, 6)  4.93 us
  transfers between devices with their start and end apart: 10, of which 3 were waited for; matrix products, arithmetic and copies ran while one was open for 13% of the time, Pallas kernels for 4%

profile of v3, /device:TPU:1, one launch (start us, length us, event | category | flops | bytes accessed | tf_op | source)
XLA Modules:
  0.0 142.4 jit_solution(5369831369558915761)
XLA Ops:
  0.0 1.7 %dynamic-slice_bitcast_fusion = (bf16[5,10,2,320]{3,2,1,0:T(2,128)(2,1)S(1)}, bf16[5,10,2,320]{3,2,1,0:T(2,128)(2,1)S(1)}, bf16[5,10,2,320]{3,2,1,0:T(2,128)(2,1...) fusion(bf16[5,8,2,2,10,320]{5,2,4,3,1,0:T(2,128)(2,1)} %bitcast, ...), kind=kLoop, calls=%fused_computation.21 | loop fusion | bytes 1024036 | tf_op jit(solution)/shard_map/jit(dynamic_index_in_dim)/squeeze | solution.py:325
  1.7 2.1 %collective-permute-start = (bf16[5,10,2,320]{3,2,1,0:T(2,128)(2,1)S(1)}, bf16[5,10,2,320]{3,2,1,0:T(2,128)(2,1)S(1)}, u32[]{:S(2)}, u32[]{:S(2)}) collective-permute-start(bf16[5,10,2,320]{3,2,1,0:T(2,128)(2,1)S(1)} %get-tuple-element.32), channel_id=1, source_target_pairs={{0,2},{2,0},{4,6},{6,4},{8,10},{10,8},{12,14},{14,12},{1,3},{3,1},... | collective-permute-start | bytes 192008 | tf_op jit(solution)/shard_map/ppermute | solution.py:327
  3.8 1.3 collective-permute-start.1
  5.1 2.4 %collective-permute-start.3 = (bf16[5,10,2,320]{3,2,1,0:T(2,128)(2,1)S(1)}, bf16[5,10,2,320]{3,2,1,0:T(2,128)(2,1)S(1)}, u32[]{:S(2)}, u32[]{:S(2)}) collective-permute-start(bf16[5,10,2,320]{3,2,1,0:T(2,128)(2,1)S(1)} %get-tuple-element.29), channel_id=1, source_target_pairs={{0,8},{2,10},{4,12},{6,14},{8,0},{10,2},{12,4},{14,6},{1,9},{3,11}... | collective-permute-start | bytes 192008 | tf_op jit(solution)/shard_map/ppermute | solution.py:327
  7.5 1.0 collective-permute-start.4
  8.5 3.3 %collective-permute-start.5 = (bf16[5,10,2,320]{3,2,1,0:T(2,128)(2,1)S(1)}, bf16[5,10,2,320]{3,2,1,0:T(2,128)(2,1)S(1)}, u32[]{:S(2)}, u32[]{:S(2)}) collective-permute-start(bf16[5,10,2,320]{3,2,1,0:T(2,128)(2,1)S(1)} %get-tuple-element.34), channel_id=1, source_target_pairs={{0,12},{2,14},{4,8},{6,10},{8,4},{10,6},{12,0},{14,2},{1,13},{3,15... | collective-permute-start | bytes 192008 | tf_op jit(solution)/shard_map/ppermute | solution.py:327
  11.9 1.5 %copy-done.1 = bf16[22,8,8,640]{3,2,1,0:T(8,128)(2,1)S(1)} copy-done((bf16[22,8,8,640]{3,2,1,0:T(8,128)(2,1)S(1)}, bf16[22,8,8,640]{3,2,1,0:T(8,128)(2,1)}, u32[]{:S(2)}) %copy-start.1) | copy-done | bytes 1802264
  13.4 3.1 %pack.1 = bf16[8,2,88,640]{3,2,1,0:T(8,128)(2,1)} custom-call(bf16[704,704]{1,0:T(8,128)(2,1)S(1)} %copy-done.3, bf16[22,8,8,640]{3,2,1,0:T(8,128)(2,1)S(1)} %copy-done.1), custom_call_target="tpu_custom_call" | custom-call | tf_op jit(solution)/shard_map/pack/pallas_call | solution.py:206
  16.5 2.5 %collective-permute-done.4 = bf16[5,10,2,320]{3,2,1,0:T(2,128)(2,1)S(1)} collective-permute-done((bf16[5,10,2,320]{3,2,1,0:T(2,128)(2,1)S(1)}, bf16[5,10,2,320]{3,2,1,0:T(2,128)(2,1)S(1)}, u32[]{:S(2)}, u32[]{:S(2)}) %collective-permute-start.4) | collective-permute-done | bytes 64032 | tf_op jit(solution)/shard_map/ppermute | solution.py:327
  20.5 8.3 %all-to-all-start = ((bf16[16,88,640]{2,1,0:T(8,128)(2,1)}), bf16[16,88,640]{2,1,0:T(8,128)(2,1)}, u32[]{:S(2)}, u32[]{:S(2)}) async-start(bf16[16,88,640]{2,1,0:T(8,128)(2,1)} %bitcast.17), calls=%async_computation | async-start | bytes 3604480 | tf_op jit(solution)/shard_map/all_to_all | solution.py:344
  29.8 1.3 collective-permute-start.7
  31.0 14.2 %collective-permute-done.7 = bf16[8,5,10,2,320]{4,3,2,0,1:T(2,128)(2,1)S(1)} collective-permute-done((bf16[8,5,10,2,320]{4,3,2,0,1:T(2,128)(2,1)S(1)}, bf16[8,5,10,2,320]{4,3,2,0,1:T(2,128)(2,1)S(1)}, u32[]{:S(2)}, u32[]{:S(2)}) %collective-permute-start.7) | collective-permute-done | bytes 512032 | tf_op jit(solution)/shard_map/ppermute | solution.py:299
  45.2 1.0 fusion.2
  46.2 2.8 %pad_maximum_fusion = bf16[2,8,5,10,2,320]{5,4,3,0,1,2:T(2,128)(2,1)} fusion(bf16[1,8,5,10,2,320]{5,4,3,0,1,2:T(2,128)(2,1)S(1)} %get-tuple-element.26, bf16[1,8,5,10,2,320]{5,4,3,0,1,2:T(2,128)(2,1)S(1)} %get-tuple-element.25), kind=kLoop, calls=%fused_computation.5 | loop fusion | flops 512000 | bytes 2048000 | tf_op jit(solution)/shard_map/stack | solution.py:304
  49.0 0.9 collective-permute-start.8
  50.5 2.1 %collective-permute-done.8 = bf16[2,8,5,10,2,320]{5,4,3,0,1,2:T(2,128)(2,1)S(1)} collective-permute-done((bf16[2,8,5,10,2,320]{5,4,3,0,1,2:T(2,128)(2,1)}, bf16[2,8,5,10,2,320]{5,4,3,0,1,2:T(2,128)(2,1)S(1)}, u32[]{:S(2)}, u32[]{:S(2)}) %collective-permute-start.8) | collective-permute-done | bytes 1024032 | tf_op jit(solution)/shard_map/ppermute | solution.py:299
  52.6 2.9 %fusion = (bf16[1,2,8,5,10,2,320]{6,5,4,1,0,2,3:T(2,128)(2,1)S(1)}, bf16[1,2,8,5,10,2,320]{6,5,4,1,0,2,3:T(2,128)(2,1)S(1)}) fusion(bf16[2,8,5,10,2,320]{5,4,3,0,1,2:T(2,128)(2,1)S(1)} %collective-permute-done.8, pred[]{:T(512)S(6)} %eq.15, bf16[1,8,5,10,2,320]{5,4,3,0,1,2:T(2,128)(2,1)S(1)} %get-tuple-element.26, ...), kind=kLoop, calls=%fused_computation.3 | loop fusion | flops 1536000 | bytes 4096001 | tf_op jit(solution)/shard_map/stack | solution.py:304
  55.5 4.9 %maximum_bitcast_fusion = bf16[5,8,2,2,10,2,320]{6,5,4,3,2,1,0:T(2,128)(2,1)} fusion(bf16[1,2,8,5,10,2,320]{6,5,4,1,0,2,3:T(2,128)(2,1)S(1)} %get-tuple-element.24, bf16[1,2,8,5,10,2,320]{6,5,4,1,0,2,3:T(2,128)(2,1)S(1)} %get-tuple-element.23), kind=kLoop, calls=%fused_computation | loop fusion | flops 1024000 | bytes 4096000 | tf_op jit(solution)/shard_map/transpose | solution.py:354
  60.5 5.0 %reshape.38.in_ref = bf16[5,320,640]{2,1,0:T(8,128)(2,1)S(1)} reshape(bf16[5,8,2,2,10,2,320]{6,5,4,3,2,1,0:T(2,128)(2,1)} %maximum_bitcast_fusion) | data formatting | bytes 4096000 | tf_op jit(solution)/shard_map/reshape | solution.py:357
  65.5 2.2 %real_form.1.rest_1_ = bf16[3200,640]{1,0:T(8,128)(2,1)S(1)} custom-call(bf16[5,320,640]{2,1,0:T(8,128)(2,1)S(1)} %reshape.38.in_ref), custom_call_target="tpu_custom_call" | custom-call | tf_op jit(solution)/shard_map/real_form/pallas_call | solution.py:250
  67.7 1.9 %copy-done = bf16[3200,640]{1,0:T(8,128)(2,1)} copy-done((bf16[3200,640]{1,0:T(8,128)(2,1)}, bf16[3200,640]{1,0:T(8,128)(2,1)S(1)}, u32[]{:S(2)}) %copy-start) | copy-done | bytes 4096024
  69.7 20.9 %couple.1 = bf16[16,88,640]{2,1,0:T(8,128)(2,1)} custom-call(s32[16,5]{1,0:T(8,128)} %copy.25.gate_ref, bf16[16,88,640]{2,1,0:T(8,128)(2,1)} %all-to-all-done.rest_0_, bf16[3200,640]{1,0:T(8,128)(2,1)} %copy-done, bf16[384,1536]{1,0:T(8,128)(2,1)} %constant.296.clone.rest_2_, bf16[384,2048]{1,0:T(8,128)(2,1)} %constant.297.clone.rest_3_, ...), custom_call_target="tpu_custom_call" | custom-call | tf_op jit(solution)/shard_map/couple/pallas_call | solution.py:174
  90.6 48.7 %all_to_all.10 = bf16[16,88,640]{2,1,0:T(8,128)(2,1)S(1)} all-to-all(bf16[16,88,640]{2,1,0:T(8,128)(2,1)} %couple.1), channel_id=1, replica_groups=mesh['group'=2,'freq'=8,'rest'=2] {'freq','rest'}, dimensions={0} | all-to-all | bytes 3604480 | tf_op jit(solution)/shard_map/all_to_all | solution.py:361
  139.3 3.1 %unpack.1 = bf16[22,8,8,640]{3,2,1,0:T(8,128)(2,1)} custom-call(bf16[704,704]{1,0:T(8,128)(2,1)S(1)} %copy-done.2, bf16[8,2,88,640]{3,2,1,0:T(8,128)(2,1)S(1)} %bitcast.83), custom_call_target="tpu_custom_call" | custom-call | tf_op jit(solution)/shard_map/unpack/pallas_call | solution.py:225
  (30 shorter events, 3.2 us)
Async XLA Ops:
  0.0 11.9 %copy-start.3 = (bf16[704,704]{1,0:T(8,128)(2,1)S(1)}, bf16[704,704]{1,0:T(8,128)(2,1)}, u32[]{:S(2)}) copy-start(bf16[704,704]{1,0:T(8,128)(2,1)} %constant.295.clone.matrix_ref) | copy-start | bytes 2973700
  1.7 6.9 %collective-permute-start = (bf16[5,10,2,320]{3,2,1,0:T(2,128)(2,1)S(1)}, bf16[5,10,2,320]{3,2,1,0:T(2,128)(2,1)S(1)}, u32[]{:S(2)}, u32[]{:S(2)}) collective-permute-start(bf16[5,10,2,320]{3,2,1,0:T(2,128)(2,1)S(1)} %get-tuple-element.32), channel_id=1, source_target_pairs={{0,2},{2,0},{4,6},{6,4},{8,10},{10,8},{12,14},{14,12},{1,3},{3,1},... | collective-permute-start | bytes 192008 | tf_op jit(solution)/shard_map/ppermute | solution.py:327
  3.8 8.1 %collective-permute-start.1 = (bf16[5,10,2,320]{3,2,1,0:T(2,128)(2,1)S(1)}, bf16[5,10,2,320]{3,2,1,0:T(2,128)(2,1)S(1)}, u32[]{:S(2)}, u32[]{:S(2)}) collective-permute-start(bf16[5,10,2,320]{3,2,1,0:T(2,128)(2,1)S(1)} %get-tuple-element.31), channel_id=1, source_target_pairs={{0,4},{2,6},{4,0},{6,2},{8,12},{10,14},{12,8},{14,10},{1,5},{3,7},... | collective-permute-start | bytes 192008 | tf_op jit(solution)/shard_map/ppermute | solution.py:327
  5.1 11.4 %collective-permute-start.2 = (bf16[5,10,2,320]{3,2,1,0:T(2,128)(2,1)S(1)}, bf16[5,10,2,320]{3,2,1,0:T(2,128)(2,1)S(1)}, u32[]{:S(2)}, u32[]{:S(2)}) collective-permute-start(bf16[5,10,2,320]{3,2,1,0:T(2,128)(2,1)S(1)} %get-tuple-element.30), channel_id=1, source_target_pairs={{0,6},{2,4},{4,2},{6,0},{8,14},{10,12},{12,10},{14,8},{1,7},{3,5},... | collective-permute-start | bytes 192008 | tf_op jit(solution)/shard_map/ppermute | solution.py:327
  5.1 11.4 %collective-permute-start.3 = (bf16[5,10,2,320]{3,2,1,0:T(2,128)(2,1)S(1)}, bf16[5,10,2,320]{3,2,1,0:T(2,128)(2,1)S(1)}, u32[]{:S(2)}, u32[]{:S(2)}) collective-permute-start(bf16[5,10,2,320]{3,2,1,0:T(2,128)(2,1)S(1)} %get-tuple-element.29), channel_id=1, source_target_pairs={{0,8},{2,10},{4,12},{6,14},{8,0},{10,2},{12,4},{14,6},{1,9},{3,11}... | collective-permute-start | bytes 192008 | tf_op jit(solution)/shard_map/ppermute | solution.py:327
  7.5 11.5 %collective-permute-start.4 = (bf16[5,10,2,320]{3,2,1,0:T(2,128)(2,1)S(1)}, bf16[5,10,2,320]{3,2,1,0:T(2,128)(2,1)S(1)}, u32[]{:S(2)}, u32[]{:S(2)}) collective-permute-start(bf16[5,10,2,320]{3,2,1,0:T(2,128)(2,1)S(1)} %get-tuple-element.28), channel_id=1, source_target_pairs={{0,10},{2,8},{4,14},{6,12},{8,2},{10,0},{12,6},{14,4},{1,11},{3,9}... | collective-permute-start | bytes 192008 | tf_op jit(solution)/shard_map/ppermute | solution.py:327
  8.5 10.4 %collective-permute-start.5 = (bf16[5,10,2,320]{3,2,1,0:T(2,128)(2,1)S(1)}, bf16[5,10,2,320]{3,2,1,0:T(2,128)(2,1)S(1)}, u32[]{:S(2)}, u32[]{:S(2)}) collective-permute-start(bf16[5,10,2,320]{3,2,1,0:T(2,128)(2,1)S(1)} %get-tuple-element.34), channel_id=1, source_target_pairs={{0,12},{2,14},{4,8},{6,10},{8,4},{10,6},{12,0},{14,2},{1,13},{3,15... | collective-permute-start | bytes 192008 | tf_op jit(solution)/shard_map/ppermute | solution.py:327
  11.9 7.1 %collective-permute-start.6 = (bf16[5,10,2,320]{3,2,1,0:T(2,128)(2,1)S(1)}, bf16[5,10,2,320]{3,2,1,0:T(2,128)(2,1)S(1)}, u32[]{:S(2)}, u32[]{:S(2)}) collective-permute-start(bf16[5,10,2,320]{3,2,1,0:T(2,128)(2,1)S(1)} %get-tuple-element.27), channel_id=1, source_target_pairs={{0,14},{2,12},{4,10},{6,8},{8,6},{10,4},{12,2},{14,0},{1,15},{3,13... | collective-permute-start | bytes 192008 | tf_op jit(solution)/shard_map/ppermute | solution.py:327
  11.9 1.5 %copy-start.1 = (bf16[22,8,8,640]{3,2,1,0:T(8,128)(2,1)S(1)}, bf16[22,8,8,640]{3,2,1,0:T(8,128)(2,1)}, u32[]{:S(2)}) copy-start(bf16[22,8,8,640]{3,2,1,0:T(8,128)(2,1)} %in_ref.1) | copy-start | bytes 5406724
  20.5 49.1 %all-to-all-start = ((bf16[16,88,640]{2,1,0:T(8,128)(2,1)}), bf16[16,88,640]{2,1,0:T(8,128)(2,1)}, u32[]{:S(2)}, u32[]{:S(2)}) async-start(bf16[16,88,640]{2,1,0:T(8,128)(2,1)} %bitcast.17), calls=%async_computation | async-start | bytes 3604480 | tf_op jit(solution)/shard_map/all_to_all | solution.py:344
  29.8 15.5 %collective-permute-start.7 = (bf16[8,5,10,2,320]{4,3,2,0,1:T(2,128)(2,1)S(1)}, bf16[8,5,10,2,320]{4,3,2,0,1:T(2,128)(2,1)S(1)}, u32[]{:S(2)}, u32[]{:S(2)}) collective-permute-start(bf16[8,5,10,2,320]{4,3,2,0,1:T(2,128)(2,1)S(1)} %bitcast.84), channel_id=1, source_target_pairs={{0,16},{16,0},{1,17},{17,1},{2,18},{18,2},{3,19},{19,3},{4,20},{20... | collective-permute-start | bytes 1536008 | tf_op jit(solution)/shard_map/ppermute | solution.py:299
  46.2 3.6 %copy-start.4 = (s32[16,5]{0,1:T(8,128)S(1)}, s32[16,5]{0,1:T(8,128)}, u32[]{:S(2)}) copy-start(s32[16,5]{0,1:T(8,128)} %param.15) | copy-start | bytes 964
  49.0 3.6 %collective-permute-start.8 = (bf16[2,8,5,10,2,320]{5,4,3,0,1,2:T(2,128)(2,1)}, bf16[2,8,5,10,2,320]{5,4,3,0,1,2:T(2,128)(2,1)S(1)}, u32[]{:S(2)}, u32[]{:S(2)}) collective-permute-start(bf16[2,8,5,10,2,320]{5,4,3,0,1,2:T(2,128)(2,1)} %pad_maximum_fusion), channel_id=1, source_target_pairs={{0,1},{1,0},{2,3},{3,2},{4,5},{5,4},{6,7},{7,6},{8,9},{9,8},{10,11... | collective-permute-start | bytes 3072008 | tf_op jit(solution)/shard_map/ppermute | solution.py:299
  67.7 1.9 %copy-start = (bf16[3200,640]{1,0:T(8,128)(2,1)}, bf16[3200,640]{1,0:T(8,128)(2,1)S(1)}, u32[]{:S(2)}) copy-start(bf16[3200,640]{1,0:T(8,128)(2,1)S(1)} %real_form.1.rest_1_) | copy-start | bytes 12288004
  90.6 48.7 %copy-start.2 = (bf16[704,704]{1,0:T(8,128)(2,1)S(1)}, bf16[704,704]{1,0:T(8,128)(2,1)}, u32[]{:S(2)}) copy-start(bf16[704,704]{1,0:T(8,128)(2,1)} %constant.304.clone.matrix_ref) | copy-start | bytes 2973700

commit v4 on v3

--- a/solution.py
+++ b/solution.py
@@ -81,8 +81,8 @@
 
     def body(gate_ref, *rest):
         count = 2 + 2 * items
-        far, out_ref, near = rest[:count], rest[count], rest[count + 1 : 2 * count + 1]
-        modes_ref, moved_ref, sems = rest[2 * count + 1 :]
+        far, out_hbm, near = rest[:count], rest[count], rest[count + 1 : 2 * count + 1]
+        modes_ref, moved_ref, out_ref, sems, out_sems = rest[2 * count + 1 :]
         data_ref, weight_ref = near[0], near[1]
         forward_refs, inverse_refs = near[2 : 2 + items], near[2 + items :]
         copies = [pltpu.make_async_copy(far[index], near[index], sems.at[index]) for index in range(count)]
@@ -94,6 +94,7 @@
         for index in order_of_use:
             copies[index].start()
         copies[0].wait()
+        leaving = []
         tail = None
         tail_at = 0
         for start in range(0, items, group):
@@ -131,7 +132,7 @@
                 lambda first, size: moved_ref[first : first + size].reshape(size * lines, orders * width),
                 weight_ref[...],
                 blocks,
-                4,
+                2,
             ).reshape(blocks, lines, width)
             for offset in range(group):
                 item = start + offset
@@ -153,8 +154,14 @@
                 last = item == items - 1 or spans[item + 1][0] >= high
                 stop = high if last else spans[item + 1][0]
                 out_ref[:, low:stop, :] = (result[:, : stop - low] * norm).astype(jnp.bfloat16)
+                leaving.append(
+                    pltpu.make_async_copy(out_ref.at[:, low:stop], out_hbm.at[:, low:stop], out_sems.at[item])
+                )
+                leaving[-1].start()
                 tail = None if last else result[:, stop - low :]
                 tail_at = stop
+        for copy in leaving:
+            copy.wait()
 
     return body
 
@@ -175,12 +182,14 @@
         make_kernel(blocks, items, orders, width, split, spans, group),
         out_shape=jax.ShapeDtypeStruct(data.shape, jnp.bfloat16),
         in_specs=[pl.BlockSpec(memory_space=pltpu.SMEM)] + [pl.BlockSpec(memory_space=pltpu.HBM)] * len(operands),
-        out_specs=pl.BlockSpec(memory_space=pltpu.VMEM),
+        out_specs=pl.BlockSpec(memory_space=pltpu.HBM),
         scratch_shapes=[pltpu.VMEM(operand.shape, operand.dtype) for operand in operands]
         + [
             pltpu.VMEM((blocks + orders - 1, rows, width), jnp.bfloat16),
             pltpu.VMEM((blocks, rows, orders * width), jnp.bfloat16),
+            pltpu.VMEM(data.shape, jnp.bfloat16),
             pltpu.SemaphoreType.DMA((len(operands),)),
+            pltpu.SemaphoreType.DMA((items,)),
         ],
         compiler_params=pltpu.CompilerParams(vmem_limit_bytes=60 * 1024 * 1024),
         name="couple",

time: 143 us -> 142 us (level)
  no operation moved by 1% of the time
where the time goes in v4:
time: 142 us
  blocking collectives  48.7 us (34%)
  Pallas kernels  28.5 us (20%)
  starting transfers between devices  20.6 us (15%)
  waiting for transfers between devices  18.8 us (13%)
  other arithmetic  13 us (9%)
  local copies, waits for them, and re-layouts  11.7 us (8%)
    all_to_all x1, blocking collectives, shards(): returned = lax.all_to_all(result, peers, 0, 0, tiled=True)  48.7 us
    pallas_call x1, Pallas kernels, couple(): pl.pallas_call(make_kernel(blocks, items, orders, width, split, spans, gr...  20 us
    ppermute x2, waiting for transfers between devices, swap(): return lax.ppermute(values, axis, [(0, 1), (1, 0)])  16.3 us
    ppermute x7, starting transfers between devices, shards(): got.append(lax.ppermute(block, 'freq', pairs) if step else block)  10.2 us
    all_to_all x1, starting transfers between devices, shards(): data = lax.all_to_all(packed, peers, 0, 0, tiled=True)  8.26 us
    another operation x3, other arithmetic, in_order(): jnp.stack([jnp.where(mine_first, first, other), jnp.where(mine_first, oth...  6.66 us
    reshape x1, local copies, waits for them, and re-layouts, shards(): full = full.reshape(orders, nodes * own_rows, width)  5 us
    transpose x1, other arithmetic, shards(): full = full.transpose(3, 2, 0, 1, 4, 5, 6)  4.93 us
  transfers between devices with their start and end apart: 10, of which 3 were waited for; matrix products, arithmetic and copies ran while one was open for 13% of the time, Pallas kernels for 4%

profile of v4, /device:TPU:1, one launch (start us, length us, event | category | flops | bytes accessed | tf_op | source)
XLA Modules:
  0.0 141.5 jit_solution(4826468919003394381)
XLA Ops:
  0.0 1.7 %dynamic-slice_bitcast_fusion = (bf16[5,10,2,320]{3,2,1,0:T(2,128)(2,1)S(1)}, bf16[5,10,2,320]{3,2,1,0:T(2,128)(2,1)S(1)}, bf16[5,10,2,320]{3,2,1,0:T(2,128)(2,1...) fusion(bf16[5,8,2,2,10,320]{5,2,4,3,1,0:T(2,128)(2,1)} %bitcast, ...), kind=kLoop, calls=%fused_computation.21 | loop fusion | bytes 1024036 | tf_op jit(solution)/shard_map/jit(dynamic_index_in_dim)/squeeze | solution.py:334
  1.7 2.1 %collective-permute-start = (bf16[5,10,2,320]{3,2,1,0:T(2,128)(2,1)S(1)}, bf16[5,10,2,320]{3,2,1,0:T(2,128)(2,1)S(1)}, u32[]{:S(2)}, u32[]{:S(2)}) collective-permute-start(bf16[5,10,2,320]{3,2,1,0:T(2,128)(2,1)S(1)} %get-tuple-element.32), channel_id=1, source_target_pairs={{0,2},{2,0},{4,6},{6,4},{8,10},{10,8},{12,14},{14,12},{1,3},{3,1},... | collective-permute-start | bytes 192008 | tf_op jit(solution)/shard_map/ppermute | solution.py:336
  3.8 1.3 collective-permute-start.1
  5.1 2.4 %collective-permute-start.3 = (bf16[5,10,2,320]{3,2,1,0:T(2,128)(2,1)S(1)}, bf16[5,10,2,320]{3,2,1,0:T(2,128)(2,1)S(1)}, u32[]{:S(2)}, u32[]{:S(2)}) collective-permute-start(bf16[5,10,2,320]{3,2,1,0:T(2,128)(2,1)S(1)} %get-tuple-element.29), channel_id=1, source_target_pairs={{0,8},{2,10},{4,12},{6,14},{8,0},{10,2},{12,4},{14,6},{1,9},{3,11}... | collective-permute-start | bytes 192008 | tf_op jit(solution)/shard_map/ppermute | solution.py:336
  7.5 1.0 collective-permute-start.4
  8.5 3.3 %collective-permute-start.5 = (bf16[5,10,2,320]{3,2,1,0:T(2,128)(2,1)S(1)}, bf16[5,10,2,320]{3,2,1,0:T(2,128)(2,1)S(1)}, u32[]{:S(2)}, u32[]{:S(2)}) collective-permute-start(bf16[5,10,2,320]{3,2,1,0:T(2,128)(2,1)S(1)} %get-tuple-element.34), channel_id=1, source_target_pairs={{0,12},{2,14},{4,8},{6,10},{8,4},{10,6},{12,0},{14,2},{1,13},{3,15... | collective-permute-start | bytes 192008 | tf_op jit(solution)/shard_map/ppermute | solution.py:336
  11.9 1.5 %copy-done.1 = bf16[22,8,8,640]{3,2,1,0:T(8,128)(2,1)S(1)} copy-done((bf16[22,8,8,640]{3,2,1,0:T(8,128)(2,1)S(1)}, bf16[22,8,8,640]{3,2,1,0:T(8,128)(2,1)}, u32[]{:S(2)}) %copy-start.1) | copy-done | bytes 1802264
  13.4 3.1 %pack.1 = bf16[8,2,88,640]{3,2,1,0:T(8,128)(2,1)} custom-call(bf16[704,704]{1,0:T(8,128)(2,1)S(1)} %copy-done.3, bf16[22,8,8,640]{3,2,1,0:T(8,128)(2,1)S(1)} %copy-done.1), custom_call_target="tpu_custom_call" | custom-call | tf_op jit(solution)/shard_map/pack/pallas_call | solution.py:215
  16.5 2.5 %collective-permute-done.4 = bf16[5,10,2,320]{3,2,1,0:T(2,128)(2,1)S(1)} collective-permute-done((bf16[5,10,2,320]{3,2,1,0:T(2,128)(2,1)S(1)}, bf16[5,10,2,320]{3,2,1,0:T(2,128)(2,1)S(1)}, u32[]{:S(2)}, u32[]{:S(2)}) %collective-permute-start.4) | collective-permute-done | bytes 64032 | tf_op jit(solution)/shard_map/ppermute | solution.py:336
  20.5 8.3 %all-to-all-start = ((bf16[16,88,640]{2,1,0:T(8,128)(2,1)}), bf16[16,88,640]{2,1,0:T(8,128)(2,1)}, u32[]{:S(2)}, u32[]{:S(2)}) async-start(bf16[16,88,640]{2,1,0:T(8,128)(2,1)} %bitcast.17), calls=%async_computation | async-start | bytes 3604480 | tf_op jit(solution)/shard_map/all_to_all | solution.py:353
  29.8 1.3 collective-permute-start.7
  31.0 14.2 %collective-permute-done.7 = bf16[8,5,10,2,320]{4,3,2,0,1:T(2,128)(2,1)S(1)} collective-permute-done((bf16[8,5,10,2,320]{4,3,2,0,1:T(2,128)(2,1)S(1)}, bf16[8,5,10,2,320]{4,3,2,0,1:T(2,128)(2,1)S(1)}, u32[]{:S(2)}, u32[]{:S(2)}) %collective-permute-start.7) | collective-permute-done | bytes 512032 | tf_op jit(solution)/shard_map/ppermute | solution.py:308
  45.2 1.0 fusion.2
  46.2 2.8 %pad_maximum_fusion = bf16[2,8,5,10,2,320]{5,4,3,0,1,2:T(2,128)(2,1)} fusion(bf16[1,8,5,10,2,320]{5,4,3,0,1,2:T(2,128)(2,1)S(1)} %get-tuple-element.26, bf16[1,8,5,10,2,320]{5,4,3,0,1,2:T(2,128)(2,1)S(1)} %get-tuple-element.25), kind=kLoop, calls=%fused_computation.5 | loop fusion | flops 512000 | bytes 2048000 | tf_op jit(solution)/shard_map/stack | solution.py:313
  49.0 0.9 collective-permute-start.8
  50.5 2.1 %collective-permute-done.8 = bf16[2,8,5,10,2,320]{5,4,3,0,1,2:T(2,128)(2,1)S(1)} collective-permute-done((bf16[2,8,5,10,2,320]{5,4,3,0,1,2:T(2,128)(2,1)}, bf16[2,8,5,10,2,320]{5,4,3,0,1,2:T(2,128)(2,1)S(1)}, u32[]{:S(2)}, u32[]{:S(2)}) %collective-permute-start.8) | collective-permute-done | bytes 1024032 | tf_op jit(solution)/shard_map/ppermute | solution.py:308
  52.6 2.9 %fusion = (bf16[1,2,8,5,10,2,320]{6,5,4,1,0,2,3:T(2,128)(2,1)S(1)}, bf16[1,2,8,5,10,2,320]{6,5,4,1,0,2,3:T(2,128)(2,1)S(1)}) fusion(bf16[2,8,5,10,2,320]{5,4,3,0,1,2:T(2,128)(2,1)S(1)} %collective-permute-done.8, pred[]{:T(512)S(6)} %eq.15, bf16[1,8,5,10,2,320]{5,4,3,0,1,2:T(2,128)(2,1)S(1)} %get-tuple-element.26, ...), kind=kLoop, calls=%fused_computation.3 | loop fusion | flops 1536000 | bytes 4096001 | tf_op jit(solution)/shard_map/stack | solution.py:313
  55.5 4.9 %maximum_bitcast_fusion = bf16[5,8,2,2,10,2,320]{6,5,4,3,2,1,0:T(2,128)(2,1)} fusion(bf16[1,2,8,5,10,2,320]{6,5,4,1,0,2,3:T(2,128)(2,1)S(1)} %get-tuple-element.24, bf16[1,2,8,5,10,2,320]{6,5,4,1,0,2,3:T(2,128)(2,1)S(1)} %get-tuple-element.23), kind=kLoop, calls=%fused_computation | loop fusion | flops 1024000 | bytes 4096000 | tf_op jit(solution)/shard_map/transpose | solution.py:363
  60.5 5.0 %reshape.38.in_ref = bf16[5,320,640]{2,1,0:T(8,128)(2,1)S(1)} reshape(bf16[5,8,2,2,10,2,320]{6,5,4,3,2,1,0:T(2,128)(2,1)} %maximum_bitcast_fusion) | data formatting | bytes 4096000 | tf_op jit(solution)/shard_map/reshape | solution.py:366
  65.5 2.2 %real_form.1.rest_1_ = bf16[3200,640]{1,0:T(8,128)(2,1)S(1)} custom-call(bf16[5,320,640]{2,1,0:T(8,128)(2,1)S(1)} %reshape.38.in_ref), custom_call_target="tpu_custom_call" | custom-call | tf_op jit(solution)/shard_map/real_form/pallas_call | solution.py:259
  67.7 1.9 %copy-done = bf16[3200,640]{1,0:T(8,128)(2,1)} copy-done((bf16[3200,640]{1,0:T(8,128)(2,1)}, bf16[3200,640]{1,0:T(8,128)(2,1)S(1)}, u32[]{:S(2)}) %copy-start) | copy-done | bytes 4096024
  69.7 20.0 %couple.1 = bf16[16,88,640]{2,1,0:T(8,128)(2,1)} custom-call(s32[16,5]{1,0:T(8,128)} %copy.25.gate_ref, bf16[16,88,640]{2,1,0:T(8,128)(2,1)} %all-to-all-done.rest_0_, bf16[3200,640]{1,0:T(8,128)(2,1)} %copy-done, bf16[384,1536]{1,0:T(8,128)(2,1)} %constant.296.clone.rest_2_, bf16[384,2048]{1,0:T(8,128)(2,1)} %constant.297.clone.rest_3_, ...), custom_call_target="tpu_custom_call" | custom-call | tf_op jit(solution)/shard_map/couple/pallas_call | solution.py:181
  89.7 48.7 %all_to_all.10 = bf16[16,88,640]{2,1,0:T(8,128)(2,1)S(1)} all-to-all(bf16[16,88,640]{2,1,0:T(8,128)(2,1)} %couple.1), channel_id=1, replica_groups=mesh['group'=2,'freq'=8,'rest'=2] {'freq','rest'}, dimensions={0} | all-to-all | bytes 3604480 | tf_op jit(solution)/shard_map/all_to_all | solution.py:370
  138.4 3.1 %unpack.1 = bf16[22,8,8,640]{3,2,1,0:T(8,128)(2,1)} custom-call(bf16[704,704]{1,0:T(8,128)(2,1)S(1)} %copy-done.2, bf16[8,2,88,640]{3,2,1,0:T(8,128)(2,1)S(1)} %bitcast.83), custom_call_target="tpu_custom_call" | custom-call | tf_op jit(solution)/shard_map/unpack/pallas_call | solution.py:234
  (30 shorter events, 3.2 us)
Async XLA Ops:
  0.0 11.9 %copy-start.3 = (bf16[704,704]{1,0:T(8,128)(2,1)S(1)}, bf16[704,704]{1,0:T(8,128)(2,1)}, u32[]{:S(2)}) copy-start(bf16[704,704]{1,0:T(8,128)(2,1)} %constant.295.clone.matrix_ref) | copy-start | bytes 2973700
  1.7 6.9 %collective-permute-start = (bf16[5,10,2,320]{3,2,1,0:T(2,128)(2,1)S(1)}, bf16[5,10,2,320]{3,2,1,0:T(2,128)(2,1)S(1)}, u32[]{:S(2)}, u32[]{:S(2)}) collective-permute-start(bf16[5,10,2,320]{3,2,1,0:T(2,128)(2,1)S(1)} %get-tuple-element.32), channel_id=1, source_target_pairs={{0,2},{2,0},{4,6},{6,4},{8,10},{10,8},{12,14},{14,12},{1,3},{3,1},... | collective-permute-start | bytes 192008 | tf_op jit(solution)/shard_map/ppermute | solution.py:336
  3.8 8.1 %collective-permute-start.1 = (bf16[5,10,2,320]{3,2,1,0:T(2,128)(2,1)S(1)}, bf16[5,10,2,320]{3,2,1,0:T(2,128)(2,1)S(1)}, u32[]{:S(2)}, u32[]{:S(2)}) collective-permute-start(bf16[5,10,2,320]{3,2,1,0:T(2,128)(2,1)S(1)} %get-tuple-element.31), channel_id=1, source_target_pairs={{0,4},{2,6},{4,0},{6,2},{8,12},{10,14},{12,8},{14,10},{1,5},{3,7},... | collective-permute-start | bytes 192008 | tf_op jit(solution)/shard_map/ppermute | solution.py:336
  5.1 11.4 %collective-permute-start.2 = (bf16[5,10,2,320]{3,2,1,0:T(2,128)(2,1)S(1)}, bf16[5,10,2,320]{3,2,1,0:T(2,128)(2,1)S(1)}, u32[]{:S(2)}, u32[]{:S(2)}) collective-permute-start(bf16[5,10,2,320]{3,2,1,0:T(2,128)(2,1)S(1)} %get-tuple-element.30), channel_id=1, source_target_pairs={{0,6},{2,4},{4,2},{6,0},{8,14},{10,12},{12,10},{14,8},{1,7},{3,5},... | collective-permute-start | bytes 192008 | tf_op jit(solution)/shard_map/ppermute | solution.py:336
  5.1 11.4 %collective-permute-start.3 = (bf16[5,10,2,320]{3,2,1,0:T(2,128)(2,1)S(1)}, bf16[5,10,2,320]{3,2,1,0:T(2,128)(2,1)S(1)}, u32[]{:S(2)}, u32[]{:S(2)}) collective-permute-start(bf16[5,10,2,320]{3,2,1,0:T(2,128)(2,1)S(1)} %get-tuple-element.29), channel_id=1, source_target_pairs={{0,8},{2,10},{4,12},{6,14},{8,0},{10,2},{12,4},{14,6},{1,9},{3,11}... | collective-permute-start | bytes 192008 | tf_op jit(solution)/shard_map/ppermute | solution.py:336
  7.5 11.5 %collective-permute-start.4 = (bf16[5,10,2,320]{3,2,1,0:T(2,128)(2,1)S(1)}, bf16[5,10,2,320]{3,2,1,0:T(2,128)(2,1)S(1)}, u32[]{:S(2)}, u32[]{:S(2)}) collective-permute-start(bf16[5,10,2,320]{3,2,1,0:T(2,128)(2,1)S(1)} %get-tuple-element.28), channel_id=1, source_target_pairs={{0,10},{2,8},{4,14},{6,12},{8,2},{10,0},{12,6},{14,4},{1,11},{3,9}... | collective-permute-start | bytes 192008 | tf_op jit(solution)/shard_map/ppermute | solution.py:336
  8.5 10.4 %collective-permute-start.5 = (bf16[5,10,2,320]{3,2,1,0:T(2,128)(2,1)S(1)}, bf16[5,10,2,320]{3,2,1,0:T(2,128)(2,1)S(1)}, u32[]{:S(2)}, u32[]{:S(2)}) collective-permute-start(bf16[5,10,2,320]{3,2,1,0:T(2,128)(2,1)S(1)} %get-tuple-element.34), channel_id=1, source_target_pairs={{0,12},{2,14},{4,8},{6,10},{8,4},{10,6},{12,0},{14,2},{1,13},{3,15... | collective-permute-start | bytes 192008 | tf_op jit(solution)/shard_map/ppermute | solution.py:336
  11.9 7.1 %collective-permute-start.6 = (bf16[5,10,2,320]{3,2,1,0:T(2,128)(2,1)S(1)}, bf16[5,10,2,320]{3,2,1,0:T(2,128)(2,1)S(1)}, u32[]{:S(2)}, u32[]{:S(2)}) collective-permute-start(bf16[5,10,2,320]{3,2,1,0:T(2,128)(2,1)S(1)} %get-tuple-element.27), channel_id=1, source_target_pairs={{0,14},{2,12},{4,10},{6,8},{8,6},{10,4},{12,2},{14,0},{1,15},{3,13... | collective-permute-start | bytes 192008 | tf_op jit(solution)/shard_map/ppermute | solution.py:336
  11.9 1.5 %copy-start.1 = (bf16[22,8,8,640]{3,2,1,0:T(8,128)(2,1)S(1)}, bf16[22,8,8,640]{3,2,1,0:T(8,128)(2,1)}, u32[]{:S(2)}) copy-start(bf16[22,8,8,640]{3,2,1,0:T(8,128)(2,1)} %in_ref.1) | copy-start | bytes 5406724
  20.5 49.1 %all-to-all-start = ((bf16[16,88,640]{2,1,0:T(8,128)(2,1)}), bf16[16,88,640]{2,1,0:T(8,128)(2,1)}, u32[]{:S(2)}, u32[]{:S(2)}) async-start(bf16[16,88,640]{2,1,0:T(8,128)(2,1)} %bitcast.17), calls=%async_computation | async-start | bytes 3604480 | tf_op jit(solution)/shard_map/all_to_all | solution.py:353
  29.8 15.5 %collective-permute-start.7 = (bf16[8,5,10,2,320]{4,3,2,0,1:T(2,128)(2,1)S(1)}, bf16[8,5,10,2,320]{4,3,2,0,1:T(2,128)(2,1)S(1)}, u32[]{:S(2)}, u32[]{:S(2)}) collective-permute-start(bf16[8,5,10,2,320]{4,3,2,0,1:T(2,128)(2,1)S(1)} %bitcast.84), channel_id=1, source_target_pairs={{0,16},{16,0},{1,17},{17,1},{2,18},{18,2},{3,19},{19,3},{4,20},{20... | collective-permute-start | bytes 1536008 | tf_op jit(solution)/shard_map/ppermute | solution.py:308
  46.2 3.6 %copy-start.4 = (s32[16,5]{0,1:T(8,128)S(1)}, s32[16,5]{0,1:T(8,128)}, u32[]{:S(2)}) copy-start(s32[16,5]{0,1:T(8,128)} %param.15) | copy-start | bytes 964
  49.0 3.6 %collective-permute-start.8 = (bf16[2,8,5,10,2,320]{5,4,3,0,1,2:T(2,128)(2,1)}, bf16[2,8,5,10,2,320]{5,4,3,0,1,2:T(2,128)(2,1)S(1)}, u32[]{:S(2)}, u32[]{:S(2)}) collective-permute-start(bf16[2,8,5,10,2,320]{5,4,3,0,1,2:T(2,128)(2,1)} %pad_maximum_fusion), channel_id=1, source_target_pairs={{0,1},{1,0},{2,3},{3,2},{4,5},{5,4},{6,7},{7,6},{8,9},{9,8},{10,11... | collective-permute-start | bytes 3072008 | tf_op jit(solution)/shard_map/ppermute | solution.py:308
  67.7 1.9 %copy-start = (bf16[3200,640]{1,0:T(8,128)(2,1)}, bf16[3200,640]{1,0:T(8,128)(2,1)S(1)}, u32[]{:S(2)}) copy-start(bf16[3200,640]{1,0:T(8,128)(2,1)S(1)} %real_form.1.rest_1_) | copy-start | bytes 12288004
  89.7 48.7 %copy-start.2 = (bf16[704,704]{1,0:T(8,128)(2,1)S(1)}, bf16[704,704]{1,0:T(8,128)(2,1)}, u32[]{:S(2)}) copy-start(bf16[704,704]{1,0:T(8,128)(2,1)} %constant.304.clone.matrix_ref) | copy-start | bytes 2973700

commit v5 on v4

--- a/solution.py
+++ b/solution.py
@@ -204,7 +204,9 @@
 
 def reorder_body(matrix_ref, in_ref, out_ref):
     width = in_ref.shape[-1]
-    moved = jnp.dot(matrix_ref[...], in_ref[...].reshape(-1, width), preferred_element_type=jnp.float32)
+    moved = product(
+        lambda first, size: matrix_ref[first : first + size], in_ref[...].reshape(-1, width), matrix_ref.shape[0], 2
+    )
     out_ref[...] = moved.astype(jnp.bfloat16).reshape(out_ref.shape)
 
 

time: 142 us -> 142 us (level)
  no operation moved by 1% of the time
where the time goes in v5:
time: 142 us
  blocking collectives  48.7 us (34%)
  Pallas kernels  28.5 us (20%)
  starting transfers between devices  20.6 us (15%)
  waiting for transfers between devices  18.8 us (13%)
  other arithmetic  13 us (9%)
  local copies, waits for them, and re-layouts  11.7 us (8%)
    all_to_all x1, blocking collectives, shards(): returned = lax.all_to_all(result, peers, 0, 0, tiled=True)  48.7 us
    pallas_call x1, Pallas kernels, couple(): pl.pallas_call(make_kernel(blocks, items, orders, width, split, spans, gr...  20 us
    ppermute x2, waiting for transfers between devices, swap(): return lax.ppermute(values, axis, [(0, 1), (1, 0)])  16.3 us
    ppermute x7, starting transfers between devices, shards(): got.append(lax.ppermute(block, 'freq', pairs) if step else block)  10.2 us
    all_to_all x1, starting transfers between devices, shards(): data = lax.all_to_all(packed, peers, 0, 0, tiled=True)  8.26 us
    another operation x3, other arithmetic, in_order(): jnp.stack([jnp.where(mine_first, first, other), jnp.where(mine_first, oth...  6.66 us
    reshape x1, local copies, waits for them, and re-layouts, shards(): full = full.reshape(orders, nodes * own_rows, width)  5 us
    transpose x1, other arithmetic, shards(): full = full.transpose(3, 2, 0, 1, 4, 5, 6)  4.93 us
  transfers between devices with their start and end apart: 10, of which 3 were waited for; matrix products, arithmetic and copies ran while one was open for 13% of the time, Pallas kernels for 4%

profile of v5, /device:TPU:1, one launch (start us, length us, event | category | flops | bytes accessed | tf_op | source)
XLA Modules:
  0.0 141.5 jit_solution(11602680216994988555)
XLA Ops:
  0.0 1.7 %dynamic-slice_bitcast_fusion = (bf16[5,10,2,320]{3,2,1,0:T(2,128)(2,1)S(1)}, bf16[5,10,2,320]{3,2,1,0:T(2,128)(2,1)S(1)}, bf16[5,10,2,320]{3,2,1,0:T(2,128)(2,1...) fusion(bf16[5,8,2,2,10,320]{5,2,4,3,1,0:T(2,128)(2,1)} %bitcast, ...), kind=kLoop, calls=%fused_computation.21 | loop fusion | bytes 1024036 | tf_op jit(solution)/shard_map/jit(dynamic_index_in_dim)/squeeze | solution.py:336
  1.7 2.1 %collective-permute-start = (bf16[5,10,2,320]{3,2,1,0:T(2,128)(2,1)S(1)}, bf16[5,10,2,320]{3,2,1,0:T(2,128)(2,1)S(1)}, u32[]{:S(2)}, u32[]{:S(2)}) collective-permute-start(bf16[5,10,2,320]{3,2,1,0:T(2,128)(2,1)S(1)} %get-tuple-element.32), channel_id=1, source_target_pairs={{0,2},{2,0},{4,6},{6,4},{8,10},{10,8},{12,14},{14,12},{1,3},{3,1},... | collective-permute-start | bytes 192008 | tf_op jit(solution)/shard_map/ppermute | solution.py:338
  3.8 1.3 collective-permute-start.1
  5.1 2.4 %collective-permute-start.3 = (bf16[5,10,2,320]{3,2,1,0:T(2,128)(2,1)S(1)}, bf16[5,10,2,320]{3,2,1,0:T(2,128)(2,1)S(1)}, u32[]{:S(2)}, u32[]{:S(2)}) collective-permute-start(bf16[5,10,2,320]{3,2,1,0:T(2,128)(2,1)S(1)} %get-tuple-element.29), channel_id=1, source_target_pairs={{0,8},{2,10},{4,12},{6,14},{8,0},{10,2},{12,4},{14,6},{1,9},{3,11}... | collective-permute-start | bytes 192008 | tf_op jit(solution)/shard_map/ppermute | solution.py:338
  7.5 1.0 collective-permute-start.4
  8.5 3.3 %collective-permute-start.5 = (bf16[5,10,2,320]{3,2,1,0:T(2,128)(2,1)S(1)}, bf16[5,10,2,320]{3,2,1,0:T(2,128)(2,1)S(1)}, u32[]{:S(2)}, u32[]{:S(2)}) collective-permute-start(bf16[5,10,2,320]{3,2,1,0:T(2,128)(2,1)S(1)} %get-tuple-element.34), channel_id=1, source_target_pairs={{0,12},{2,14},{4,8},{6,10},{8,4},{10,6},{12,0},{14,2},{1,13},{3,15... | collective-permute-start | bytes 192008 | tf_op jit(solution)/shard_map/ppermute | solution.py:338
  11.9 1.5 %copy-done.1 = bf16[22,8,8,640]{3,2,1,0:T(8,128)(2,1)S(1)} copy-done((bf16[22,8,8,640]{3,2,1,0:T(8,128)(2,1)S(1)}, bf16[22,8,8,640]{3,2,1,0:T(8,128)(2,1)}, u32[]{:S(2)}) %copy-start.1) | copy-done | bytes 1802264
  13.4 3.1 %pack.1 = bf16[8,2,88,640]{3,2,1,0:T(8,128)(2,1)} custom-call(bf16[704,704]{1,0:T(8,128)(2,1)S(1)} %copy-done.3, bf16[22,8,8,640]{3,2,1,0:T(8,128)(2,1)S(1)} %copy-done.1), custom_call_target="tpu_custom_call" | custom-call | tf_op jit(solution)/shard_map/pack/pallas_call | solution.py:217
  16.5 2.5 %collective-permute-done.4 = bf16[5,10,2,320]{3,2,1,0:T(2,128)(2,1)S(1)} collective-permute-done((bf16[5,10,2,320]{3,2,1,0:T(2,128)(2,1)S(1)}, bf16[5,10,2,320]{3,2,1,0:T(2,128)(2,1)S(1)}, u32[]{:S(2)}, u32[]{:S(2)}) %collective-permute-start.4) | collective-permute-done | bytes 64032 | tf_op jit(solution)/shard_map/ppermute | solution.py:338
  20.5 8.3 %all-to-all-start = ((bf16[16,88,640]{2,1,0:T(8,128)(2,1)}), bf16[16,88,640]{2,1,0:T(8,128)(2,1)}, u32[]{:S(2)}, u32[]{:S(2)}) async-start(bf16[16,88,640]{2,1,0:T(8,128)(2,1)} %bitcast.17), calls=%async_computation | async-start | bytes 3604480 | tf_op jit(solution)/shard_map/all_to_all | solution.py:355
  29.8 1.3 collective-permute-start.7
  31.0 14.2 %collective-permute-done.7 = bf16[8,5,10,2,320]{4,3,2,0,1:T(2,128)(2,1)S(1)} collective-permute-done((bf16[8,5,10,2,320]{4,3,2,0,1:T(2,128)(2,1)S(1)}, bf16[8,5,10,2,320]{4,3,2,0,1:T(2,128)(2,1)S(1)}, u32[]{:S(2)}, u32[]{:S(2)}) %collective-permute-start.7) | collective-permute-done | bytes 512032 | tf_op jit(solution)/shard_map/ppermute | solution.py:310
  45.2 1.0 fusion.2
  46.2 2.8 %pad_maximum_fusion = bf16[2,8,5,10,2,320]{5,4,3,0,1,2:T(2,128)(2,1)} fusion(bf16[1,8,5,10,2,320]{5,4,3,0,1,2:T(2,128)(2,1)S(1)} %get-tuple-element.26, bf16[1,8,5,10,2,320]{5,4,3,0,1,2:T(2,128)(2,1)S(1)} %get-tuple-element.25), kind=kLoop, calls=%fused_computation.5 | loop fusion | flops 512000 | bytes 2048000 | tf_op jit(solution)/shard_map/stack | solution.py:315
  49.0 0.9 collective-permute-start.8
  50.5 2.1 %collective-permute-done.8 = bf16[2,8,5,10,2,320]{5,4,3,0,1,2:T(2,128)(2,1)S(1)} collective-permute-done((bf16[2,8,5,10,2,320]{5,4,3,0,1,2:T(2,128)(2,1)}, bf16[2,8,5,10,2,320]{5,4,3,0,1,2:T(2,128)(2,1)S(1)}, u32[]{:S(2)}, u32[]{:S(2)}) %collective-permute-start.8) | collective-permute-done | bytes 1024032 | tf_op jit(solution)/shard_map/ppermute | solution.py:310
  52.6 2.9 %fusion = (bf16[1,2,8,5,10,2,320]{6,5,4,1,0,2,3:T(2,128)(2,1)S(1)}, bf16[1,2,8,5,10,2,320]{6,5,4,1,0,2,3:T(2,128)(2,1)S(1)}) fusion(bf16[2,8,5,10,2,320]{5,4,3,0,1,2:T(2,128)(2,1)S(1)} %collective-permute-done.8, pred[]{:T(512)S(6)} %eq.15, bf16[1,8,5,10,2,320]{5,4,3,0,1,2:T(2,128)(2,1)S(1)} %get-tuple-element.26, ...), kind=kLoop, calls=%fused_computation.3 | loop fusion | flops 1536000 | bytes 4096001 | tf_op jit(solution)/shard_map/stack | solution.py:315
  55.5 4.9 %maximum_bitcast_fusion = bf16[5,8,2,2,10,2,320]{6,5,4,3,2,1,0:T(2,128)(2,1)} fusion(bf16[1,2,8,5,10,2,320]{6,5,4,1,0,2,3:T(2,128)(2,1)S(1)} %get-tuple-element.24, bf16[1,2,8,5,10,2,320]{6,5,4,1,0,2,3:T(2,128)(2,1)S(1)} %get-tuple-element.23), kind=kLoop, calls=%fused_computation | loop fusion | flops 1024000 | bytes 4096000 | tf_op jit(solution)/shard_map/transpose | solution.py:365
  60.5 5.0 %reshape.38.in_ref = bf16[5,320,640]{2,1,0:T(8,128)(2,1)S(1)} reshape(bf16[5,8,2,2,10,2,320]{6,5,4,3,2,1,0:T(2,128)(2,1)} %maximum_bitcast_fusion) | data formatting | bytes 4096000 | tf_op jit(solution)/shard_map/reshape | solution.py:368
  65.5 2.2 %real_form.1.rest_1_ = bf16[3200,640]{1,0:T(8,128)(2,1)S(1)} custom-call(bf16[5,320,640]{2,1,0:T(8,128)(2,1)S(1)} %reshape.38.in_ref), custom_call_target="tpu_custom_call" | custom-call | tf_op jit(solution)/shard_map/real_form/pallas_call | solution.py:261
  67.7 1.9 %copy-done = bf16[3200,640]{1,0:T(8,128)(2,1)} copy-done((bf16[3200,640]{1,0:T(8,128)(2,1)}, bf16[3200,640]{1,0:T(8,128)(2,1)S(1)}, u32[]{:S(2)}) %copy-start) | copy-done | bytes 4096024
  69.7 20.0 %couple.1 = bf16[16,88,640]{2,1,0:T(8,128)(2,1)} custom-call(s32[16,5]{1,0:T(8,128)} %copy.25.gate_ref, bf16[16,88,640]{2,1,0:T(8,128)(2,1)} %all-to-all-done.rest_0_, bf16[3200,640]{1,0:T(8,128)(2,1)} %copy-done, bf16[384,1536]{1,0:T(8,128)(2,1)} %constant.296.clone.rest_2_, bf16[384,2048]{1,0:T(8,128)(2,1)} %constant.297.clone.rest_3_, ...), custom_call_target="tpu_custom_call" | custom-call | tf_op jit(solution)/shard_map/couple/pallas_call | solution.py:181
  89.7 48.7 %all_to_all.10 = bf16[16,88,640]{2,1,0:T(8,128)(2,1)S(1)} all-to-all(bf16[16,88,640]{2,1,0:T(8,128)(2,1)} %couple.1), channel_id=1, replica_groups=mesh['group'=2,'freq'=8,'rest'=2] {'freq','rest'}, dimensions={0} | all-to-all | bytes 3604480 | tf_op jit(solution)/shard_map/all_to_all | solution.py:372
  138.4 3.1 %unpack.1 = bf16[22,8,8,640]{3,2,1,0:T(8,128)(2,1)} custom-call(bf16[704,704]{1,0:T(8,128)(2,1)S(1)} %copy-done.2, bf16[8,2,88,640]{3,2,1,0:T(8,128)(2,1)S(1)} %bitcast.83), custom_call_target="tpu_custom_call" | custom-call | tf_op jit(solution)/shard_map/unpack/pallas_call | solution.py:236
  (30 shorter events, 3.2 us)
Async XLA Ops:
  0.0 11.9 %copy-start.3 = (bf16[704,704]{1,0:T(8,128)(2,1)S(1)}, bf16[704,704]{1,0:T(8,128)(2,1)}, u32[]{:S(2)}) copy-start(bf16[704,704]{1,0:T(8,128)(2,1)} %constant.295.clone.matrix_ref) | copy-start | bytes 2973700
  1.7 6.9 %collective-permute-start = (bf16[5,10,2,320]{3,2,1,0:T(2,128)(2,1)S(1)}, bf16[5,10,2,320]{3,2,1,0:T(2,128)(2,1)S(1)}, u32[]{:S(2)}, u32[]{:S(2)}) collective-permute-start(bf16[5,10,2,320]{3,2,1,0:T(2,128)(2,1)S(1)} %get-tuple-element.32), channel_id=1, source_target_pairs={{0,2},{2,0},{4,6},{6,4},{8,10},{10,8},{12,14},{14,12},{1,3},{3,1},... | collective-permute-start | bytes 192008 | tf_op jit(solution)/shard_map/ppermute | solution.py:338
  3.8 8.1 %collective-permute-start.1 = (bf16[5,10,2,320]{3,2,1,0:T(2,128)(2,1)S(1)}, bf16[5,10,2,320]{3,2,1,0:T(2,128)(2,1)S(1)}, u32[]{:S(2)}, u32[]{:S(2)}) collective-permute-start(bf16[5,10,2,320]{3,2,1,0:T(2,128)(2,1)S(1)} %get-tuple-element.31), channel_id=1, source_target_pairs={{0,4},{2,6},{4,0},{6,2},{8,12},{10,14},{12,8},{14,10},{1,5},{3,7},... | collective-permute-start | bytes 192008 | tf_op jit(solution)/shard_map/ppermute | solution.py:338
  5.1 11.4 %collective-permute-start.2 = (bf16[5,10,2,320]{3,2,1,0:T(2,128)(2,1)S(1)}, bf16[5,10,2,320]{3,2,1,0:T(2,128)(2,1)S(1)}, u32[]{:S(2)}, u32[]{:S(2)}) collective-permute-start(bf16[5,10,2,320]{3,2,1,0:T(2,128)(2,1)S(1)} %get-tuple-element.30), channel_id=1, source_target_pairs={{0,6},{2,4},{4,2},{6,0},{8,14},{10,12},{12,10},{14,8},{1,7},{3,5},... | collective-permute-start | bytes 192008 | tf_op jit(solution)/shard_map/ppermute | solution.py:338
  5.1 11.4 %collective-permute-start.3 = (bf16[5,10,2,320]{3,2,1,0:T(2,128)(2,1)S(1)}, bf16[5,10,2,320]{3,2,1,0:T(2,128)(2,1)S(1)}, u32[]{:S(2)}, u32[]{:S(2)}) collective-permute-start(bf16[5,10,2,320]{3,2,1,0:T(2,128)(2,1)S(1)} %get-tuple-element.29), channel_id=1, source_target_pairs={{0,8},{2,10},{4,12},{6,14},{8,0},{10,2},{12,4},{14,6},{1,9},{3,11}... | collective-permute-start | bytes 192008 | tf_op jit(solution)/shard_map/ppermute | solution.py:338
  7.5 11.5 %collective-permute-start.4 = (bf16[5,10,2,320]{3,2,1,0:T(2,128)(2,1)S(1)}, bf16[5,10,2,320]{3,2,1,0:T(2,128)(2,1)S(1)}, u32[]{:S(2)}, u32[]{:S(2)}) collective-permute-start(bf16[5,10,2,320]{3,2,1,0:T(2,128)(2,1)S(1)} %get-tuple-element.28), channel_id=1, source_target_pairs={{0,10},{2,8},{4,14},{6,12},{8,2},{10,0},{12,6},{14,4},{1,11},{3,9}... | collective-permute-start | bytes 192008 | tf_op jit(solution)/shard_map/ppermute | solution.py:338
  8.5 10.4 %collective-permute-start.5 = (bf16[5,10,2,320]{3,2,1,0:T(2,128)(2,1)S(1)}, bf16[5,10,2,320]{3,2,1,0:T(2,128)(2,1)S(1)}, u32[]{:S(2)}, u32[]{:S(2)}) collective-permute-start(bf16[5,10,2,320]{3,2,1,0:T(2,128)(2,1)S(1)} %get-tuple-element.34), channel_id=1, source_target_pairs={{0,12},{2,14},{4,8},{6,10},{8,4},{10,6},{12,0},{14,2},{1,13},{3,15... | collective-permute-start | bytes 192008 | tf_op jit(solution)/shard_map/ppermute | solution.py:338
  11.9 7.1 %collective-permute-start.6 = (bf16[5,10,2,320]{3,2,1,0:T(2,128)(2,1)S(1)}, bf16[5,10,2,320]{3,2,1,0:T(2,128)(2,1)S(1)}, u32[]{:S(2)}, u32[]{:S(2)}) collective-permute-start(bf16[5,10,2,320]{3,2,1,0:T(2,128)(2,1)S(1)} %get-tuple-element.27), channel_id=1, source_target_pairs={{0,14},{2,12},{4,10},{6,8},{8,6},{10,4},{12,2},{14,0},{1,15},{3,13... | collective-permute-start | bytes 192008 | tf_op jit(solution)/shard_map/ppermute | solution.py:338
  11.9 1.5 %copy-start.1 = (bf16[22,8,8,640]{3,2,1,0:T(8,128)(2,1)S(1)}, bf16[22,8,8,640]{3,2,1,0:T(8,128)(2,1)}, u32[]{:S(2)}) copy-start(bf16[22,8,8,640]{3,2,1,0:T(8,128)(2,1)} %in_ref.1) | copy-start | bytes 5406724
  20.5 49.1 %all-to-all-start = ((bf16[16,88,640]{2,1,0:T(8,128)(2,1)}), bf16[16,88,640]{2,1,0:T(8,128)(2,1)}, u32[]{:S(2)}, u32[]{:S(2)}) async-start(bf16[16,88,640]{2,1,0:T(8,128)(2,1)} %bitcast.17), calls=%async_computation | async-start | bytes 3604480 | tf_op jit(solution)/shard_map/all_to_all | solution.py:355
  29.8 15.5 %collective-permute-start.7 = (bf16[8,5,10,2,320]{4,3,2,0,1:T(2,128)(2,1)S(1)}, bf16[8,5,10,2,320]{4,3,2,0,1:T(2,128)(2,1)S(1)}, u32[]{:S(2)}, u32[]{:S(2)}) collective-permute-start(bf16[8,5,10,2,320]{4,3,2,0,1:T(2,128)(2,1)S(1)} %bitcast.84), channel_id=1, source_target_pairs={{0,16},{16,0},{1,17},{17,1},{2,18},{18,2},{3,19},{19,3},{4,20},{20... | collective-permute-start | bytes 1536008 | tf_op jit(solution)/shard_map/ppermute | solution.py:310
  46.2 3.6 %copy-start.4 = (s32[16,5]{0,1:T(8,128)S(1)}, s32[16,5]{0,1:T(8,128)}, u32[]{:S(2)}) copy-start(s32[16,5]{0,1:T(8,128)} %param.15) | copy-start | bytes 964
  49.0 3.6 %collective-permute-start.8 = (bf16[2,8,5,10,2,320]{5,4,3,0,1,2:T(2,128)(2,1)}, bf16[2,8,5,10,2,320]{5,4,3,0,1,2:T(2,128)(2,1)S(1)}, u32[]{:S(2)}, u32[]{:S(2)}) collective-permute-start(bf16[2,8,5,10,2,320]{5,4,3,0,1,2:T(2,128)(2,1)} %pad_maximum_fusion), channel_id=1, source_target_pairs={{0,1},{1,0},{2,3},{3,2},{4,5},{5,4},{6,7},{7,6},{8,9},{9,8},{10,11... | collective-permute-start | bytes 3072008 | tf_op jit(solution)/shard_map/ppermute | solution.py:310
  67.7 1.9 %copy-start = (bf16[3200,640]{1,0:T(8,128)(2,1)}, bf16[3200,640]{1,0:T(8,128)(2,1)S(1)}, u32[]{:S(2)}) copy-start(bf16[3200,640]{1,0:T(8,128)(2,1)S(1)} %real_form.1.rest_1_) | copy-start | bytes 12288004
  89.7 48.7 %copy-start.2 = (bf16[704,704]{1,0:T(8,128)(2,1)S(1)}, bf16[704,704]{1,0:T(8,128)(2,1)}, u32[]{:S(2)}) copy-start(bf16[704,704]{1,0:T(8,128)(2,1)} %constant.304.clone.matrix_ref) | copy-start | bytes 2973700
